TPU v7x, 512 devices: a whole 4x8x8 slice. The times are simulated.
512 devices in a mesh: dom: 32 (over x, z), row: 16 (over y, core).
Axes of the slice: x: 4, y: 8, z: 8, core: 2. Of those that a mesh axis runs over, the one named last changes fastest.
Arguments:
- right_side: float32 [131072, 128], P(('dom', 'row')), may hold values from -6 to 6
- spikes: float32 [5, 131072, 512], P(None, ('dom', 'row')), may hold values from -0.1875 to 0.1875
- inverses: float32 [32, 1024, 1024], P('dom', 'row'), may hold values from -1 to 2
Outputs:
- solution: float32 [131072, 128], P(('dom', 'row'))
All inputs are finite; a program needn't handle non-finite values.
Results may differ from a plain program's by a relative error of at most 0.0001.
Values sent between devices are 32-bit elements; how exact they have to be, the bound alone decides.
No kernel may reach another device: no remote copies, remote signals or barrier semaphores. Data moves between devices by JAX's collectives and lax.ppermute only.
A program may use at most 64 MiB of HBM per device.

v0:
```python
import jax
import jax.numpy as jnp
from jax import lax
from jax.sharding import PartitionSpec as P

exact_mode = lax.Precision.HIGHEST


def swapped(value, axis, bit):
    return lax.ppermute(value, axis, [(i, i ^ 1 << bit) for i in range(lax.axis_size(axis))])


def shifted(value, axis, steps):
    count = lax.axis_size(axis)
    initial, last = (max(0, -steps), min(count, count - steps))
    return lax.ppermute(value, axis, [(source, source + steps) for source in range(initial, last)])


def pair_spread(solved_rows, offset_in, half_group, level_at):
    holding = offset_in == half_group
    for bit_index in range(level_at, -1, -1):
        partner = swapped(solved_rows, "dom", bit_index)
        solved_rows = jnp.where(holding, solved_rows, partner)
        holding = offset_in % (1 << bit_index) == 0
    return solved_rows


def spread_solution(solved_rows, offset_in, half_group, level_at):
    return pair_spread(solved_rows, offset_in, half_group, level_at)


def body(right_side, spikes, inverses):
    row_count = lax.axis_size("row")
    dom_at = lax.axis_index("dom")
    row_at = lax.axis_index("row")
    local_rows, columns = right_side.shape
    spike_cols = spikes.shape[2]
    tip_devices = spike_cols // local_rows
    inverse_rows = inverses[0]
    is_top = row_at < tip_devices
    is_bottom = row_at >= row_count - tip_devices
    is_holder = is_top | is_bottom
    slot_at = jnp.where(
        is_top, spike_cols + row_at * local_rows, (row_at - (row_count - tip_devices)) * local_rows
    )
    slot_at = jnp.clip(slot_at, 0, 2 * spike_cols - local_rows)
    blank = jnp.zeros((2 * spike_cols, columns), jnp.float32)
    current = right_side
    for level_at in range(spikes.shape[0]):
        half_group = 1 << level_at
        offset_in = dom_at % (2 * half_group)
        left_block = offset_in < half_group
        incoming = shifted(current, "dom", 1)
        tip_slab = jnp.where(is_top, current, incoming)
        placed = lax.dynamic_update_slice_in_dim(blank, tip_slab, slot_at, 0)
        placed = jnp.where(is_holder, placed, 0.0)
        tip_rows = lax.psum(placed, "row")
        solved_rows = jnp.dot(
            inverse_rows, tip_rows, precision=exact_mode, preferred_element_type=jnp.float32
        )
        solved_rows = spread_solution(solved_rows, offset_in, half_group, level_at)
        spike_level = spikes[level_at]
        all_rows = lax.all_gather(solved_rows, "row", axis=0, tiled=True)
        needed_half = lax.dynamic_slice_in_dim(
            all_rows, jnp.where(left_block, spike_cols, 0), spike_cols, 0
        )
        update = jnp.dot(
            spike_level, needed_half, precision=exact_mode, preferred_element_type=jnp.float32
        )
        current = current - update
    return current


def solution(mesh):
    in_specs = (P(("dom", "row"), None), P(None, ("dom", "row"), None), P("dom", "row", None))
    out_specs = P(("dom", "row"), None)
    return jax.shard_map(body, mesh=mesh, in_specs=in_specs, out_specs=out_specs, check_vma=False)
```

profile of v0, /device:TPU:1, one launch (start us, length us, event | category | flops | bytes accessed | tf_op | source)
XLA Modules:
  0.0 864.6 jit_solution(5907681829028071343)
XLA Ops:
  7.7 4.8 collective-permute-start
  12.5 1.9 collective-permute-done
  15.2 1.4 select_n.252
  17.5 123.3 %all-reduce.6.cloned.1.call-done = f32[1024,128]{0,1:T(8,128)} async-done(((f32[1024,128]{0,1:T(8,128)}), f32[1024,128]{0,1:T(8,128)}) %all-reduce.6.cloned.1.call-update) | async-done | bytes 524304 | tf_op jit(solution)/shard_map/psum | solution.py:57
  140.8 1.7 convolution_bitcast_fusion.9
  142.5 3.3 collective-permute-start.1
  147.2 18.6 %all_gather.15 = f32[1024,128]{1,0:T(8,128)S(1)} all-gather(f32[64,128]{1,0:T(8,128)S(1)} %broadcast_select_fusion.14), channel_id=1, replica_groups=mesh['dom'=32,'row'=16] {'row'}, dimensions={0}, use_global_device_ids=true | all-gather | bytes 557056 | tf_op jit(solution)/shard_map/all_gather | solution.py:63
  166.3 3.0 collective-permute-start.2
  169.3 2.7 collective-permute-done.2
  175.1 119.3 %all-reduce.8.cloned.1.call-done = f32[1024,128]{0,1:T(8,128)} async-done(((f32[1024,128]{0,1:T(8,128)}), f32[1024,128]{0,1:T(8,128)}) %all-reduce.8.cloned.1.call-update) | async-done | bytes 524304 | tf_op jit(solution)/shard_map/psum | solution.py:57
  294.3 1.7 convolution_bitcast_fusion.8
  296.1 4.3 collective-permute-start.3
  301.7 3.3 collective-permute-start.4
  306.4 19.9 %all_gather.16 = f32[1024,128]{1,0:T(8,128)S(1)} all-gather(f32[64,128]{1,0:T(8,128)S(1)} %broadcast_select_fusion.13), channel_id=1, replica_groups=mesh['dom'=32,'row'=16] {'row'}, dimensions={0}, use_global_device_ids=true | all-gather | bytes 557056 | tf_op jit(solution)/shard_map/all_gather | solution.py:63
  326.9 2.7 collective-permute-start.5
  329.6 2.7 collective-permute-done.5
  333.9 120.2 %all-reduce.10.cloned.1.call-done = f32[1024,128]{0,1:T(8,128)} async-done(((f32[1024,128]{0,1:T(8,128)}), f32[1024,128]{0,1:T(8,128)}) %all-reduce.10.cloned.1.call-update) | async-done | bytes 524304 | tf_op jit(solution)/shard_map/psum | solution.py:57
  454.1 1.7 convolution_bitcast_fusion.7
  455.8 7.7 collective-permute-start.6
  464.9 4.2 collective-permute-start.7
  470.5 2.8 collective-permute-start.8
  473.3 1.8 collective-permute-done.8
  475.1 20.6 %all_gather.17 = f32[1024,128]{1,0:T(8,128)S(1)} all-gather(f32[64,128]{1,0:T(8,128)S(1)} %broadcast_select_fusion.11), channel_id=1, replica_groups=mesh['dom'=32,'row'=16] {'row'}, dimensions={0}, use_global_device_ids=true | all-gather | bytes 557056 | tf_op jit(solution)/shard_map/all_gather | solution.py:63
  495.8 1.5 fusion.2
  497.3 2.7 collective-permute-start.9
  500.0 2.7 collective-permute-done.9
  505.7 119.9 %all-reduce.12.cloned.1.call-done = f32[1024,128]{0,1:T(8,128)} async-done(((f32[1024,128]{0,1:T(8,128)}), f32[1024,128]{0,1:T(8,128)}) %all-reduce.12.cloned.1.call-update) | async-done | bytes 524304 | tf_op jit(solution)/shard_map/psum | solution.py:57
  625.6 1.7 convolution_bitcast_fusion.6
  627.3 3.1 collective-permute-start.10
  630.4 1.5 collective-permute-done.10
  632.0 7.7 collective-permute-start.11
  641.1 4.2 collective-permute-start.12
  646.7 2.8 collective-permute-start.13
  649.5 1.8 collective-permute-done.13
  651.3 21.9 %all_gather.18 = f32[1024,128]{1,0:T(8,128)S(1)} all-gather(f32[64,128]{1,0:T(8,128)S(1)} %broadcast_select_fusion.8), channel_id=1, replica_groups=mesh['dom'=32,'row'=16] {'row'}, dimensions={0}, use_global_device_ids=true | all-gather | bytes 557056 | tf_op jit(solution)/shard_map/all_gather | solution.py:63
  673.8 2.6 collective-permute-start.14
  676.4 2.7 collective-permute-done.14
  682.1 119.8 %all-reduce.14.cloned.1.call-done = f32[1024,128]{0,1:T(8,128)} async-done(((f32[1024,128]{0,1:T(8,128)}), f32[1024,128]{0,1:T(8,128)}) %all-reduce.14.cloned.1.call-update) | async-done | bytes 524304 | tf_op jit(solution)/shard_map/psum | solution.py:57
  801.9 1.7 convolution_bitcast_fusion.5
  803.6 4.6 collective-permute-start.15
  808.2 1.5 collective-permute-done.15
  809.8 3.1 collective-permute-start.16
  812.9 1.5 collective-permute-done.16
  814.4 7.7 collective-permute-start.17
  823.5 4.2 collective-permute-start.18
  829.1 2.8 collective-permute-start.19
  831.9 2.1 collective-permute-done.19
  834.0 22.7 %all_gather.19 = f32[1024,128]{1,0:T(8,128)S(1)} all-gather(f32[64,128]{1,0:T(8,128)S(1)} %broadcast_select_fusion.4), channel_id=1, replica_groups=mesh['dom'=32,'row'=16] {'row'}, dimensions={0}, use_global_device_ids=true | all-gather | bytes 557056 | tf_op jit(solution)/shard_map/all_gather | solution.py:63
  (70 shorter events, 28.6 us)
Async XLA Ops:
  6.5 134.3 %copy-start = (f32[1,64,1024]{2,1,0:T(8,128)S(1)}, f32[1,64,1024]{2,1,0:T(8,128)}, u32[]{:S(2)}) copy-start(f32[1,64,1024]{2,1,0:T(8,128)} %param.5) | copy-start | bytes 786436
  6.5 159.2 %copy-start.1 = (f32[5,256,512]{2,1,0:T(8,128)S(1)}, f32[5,256,512]{2,1,0:T(8,128)}, u32[]{:S(2)}) copy-start(f32[5,256,512]{2,1,0:T(8,128)} %param.4) | copy-start | bytes 7864324
  6.5 134.3 %all-reduce.6.cloned.1.call-start = ((), (), s32[]{:S(2)}) async-start(), calls=%async_computation | async-start | bytes 1048576 | tf_op jit(solution)/shard_map/psum | solution.py:57
  7.7 6.8 collective-permute-start
  16.6 0.8 copy-start.3
  17.5 276.9 %all-reduce.8.cloned.1.call-start = ((), (), s32[]{:S(2)}) async-start(), calls=%async_computation.1 | async-start | bytes 1048576 | tf_op jit(solution)/shard_map/psum | solution.py:57
  142.5 4.7 collective-permute-start.1
  166.3 5.7 collective-permute-start.2
  174.2 0.8 copy-start.4
  175.0 279.1 %all-reduce.10.cloned.1.call-start = ((), (), s32[]{:S(2)}) async-start(), calls=%async_computation.2 | async-start | bytes 1048576 | tf_op jit(solution)/shard_map/psum | solution.py:57
  296.1 5.6 collective-permute-start.3
  301.7 4.6 collective-permute-start.4
  326.9 5.5 copy-start.7
  326.9 5.4 collective-permute-start.5
  333.0 0.8 copy-start.5
  333.9 291.8 %all-reduce.12.cloned.1.call-start = ((), (), s32[]{:S(2)}) async-start(), calls=%async_computation.3 | async-start | bytes 1048576 | tf_op jit(solution)/shard_map/psum | solution.py:57
  455.8 9.1 %collective-permute-start.6 = (f32[64,128]{1,0:T(8,128)S(1)}, f32[64,128]{1,0:T(8,128)S(1)}, u32[]{:S(2)}, u32[]{:S(2)}) collective-permute-start(f32[64,128]{1,0:T(8,128)S(1)} %convolution_bitcast_fusion.7), channel_id=1, source_target_pairs={{0,64},{16,80},{32,96},{48,112},{64,0},{80,16},{96,32},{112,48},{1... | collective-permute-start | bytes 98312 | tf_op jit(solution)/shard_map/ppermute | solution.py:10
  464.9 5.5 collective-permute-start.7
  470.5 4.6 collective-permute-start.8
  497.3 5.4 collective-permute-start.9
  504.8 0.8 copy-start.6
  505.7 296.2 %all-reduce.14.cloned.1.call-start = ((), (), s32[]{:S(2)}) async-start(), calls=%async_computation.4 | async-start | bytes 1048576 | tf_op jit(solution)/shard_map/psum | solution.py:57
  627.3 4.7 collective-permute-start.10
  632.0 9.1 %collective-permute-start.11 = (f32[64,128]{1,0:T(8,128)S(1)}, f32[64,128]{1,0:T(8,128)S(1)}, u32[]{:S(2)}, u32[]{:S(2)}) collective-permute-start(f32[64,128]{1,0:T(8,128)S(1)} %broadcast_select_fusion.5), channel_id=1, source_target_pairs={{0,64},{16,80},{32,96},{48,112},{64,0},{80,16},{96,32},{112,48},{1... | collective-permute-start | bytes 98312 | tf_op jit(solution)/shard_map/ppermute | solution.py:10
  641.1 5.5 collective-permute-start.12
  646.7 4.6 collective-permute-start.13
  673.8 5.2 collective-permute-start.14
  681.2 0.8 copy-start.2
  803.6 6.2 collective-permute-start.15
  809.8 4.6 collective-permute-start.16
  814.4 9.1 %collective-permute-start.17 = (f32[64,128]{1,0:T(8,128)S(1)}, f32[64,128]{1,0:T(8,128)S(1)}, u32[]{:S(2)}, u32[]{:S(2)}) collective-permute-start(f32[64,128]{1,0:T(8,128)S(1)} %broadcast_select_fusion.1), channel_id=1, source_target_pairs={{0,64},{16,80},{32,96},{48,112},{64,0},{80,16},{96,32},{112,48},{1... | collective-permute-start | bytes 98312 | tf_op jit(solution)/shard_map/ppermute | solution.py:10
  823.5 5.5 collective-permute-start.18
  829.1 4.9 collective-permute-start.19
Sparse Core Ops, SparseCore 0:
  17.6 123.1 all-reduce.5
  175.2 119.1 all-reduce.7
  334.0 120.0 all-reduce.9
  505.8 119.7 all-reduce.11
  682.2 119.6 all-reduce.13
where the time goes:
time: 866 us; the launch traced here: 865 us
  waiting for transfers between devices  637 us (74%)
  blocking collectives  104 us (12%)
  starting transfers between devices  81.9 us (9%)
  between operations  13.8 us (2%)
  local copies, waits for them, and re-layouts  12.6 us (1%)
  matrix products  12.5 us (1%)
    psum x5, waiting for transfers between devices, body(): tip_rows = lax.psum(placed, 'row')  602 us
    all_gather x5, blocking collectives, body(): all_rows = lax.all_gather(solved_rows, 'row', axis=0, tiled=True)  104 us
    ppermute x15, starting transfers between devices, swapped(): lax.ppermute(value, axis, [(i, i ^ 1 << bit) for i in range(lax.axis_size...  65.9 us
    ppermute x15, waiting for transfers between devices, swapped(): lax.ppermute(value, axis, [(i, i ^ 1 << bit) for i in range(lax.axis_size...  22.3 us
  transfers between devices with their start and end apart: 25, of which 25 were waited for; matrix products, arithmetic and copies ran while one was open for 0% of the time, Pallas kernels for 0%

commit v1 on v0

v1 whole, which is shorter than its diff:
```python
import jax
import jax.numpy as jnp
from jax import lax
from jax.sharding import Mesh
from jax.sharding import PartitionSpec as P

CHIPS, CORES = 8, 2
AXES = ("dom", "y", "c")
MODE = lax.Precision.HIGH


def flat(dom, y, c):
    return (dom * CHIPS + y) * CORES + c


def both_cores(links):
    return [(flat(*a, c), flat(*b, c)) for a, b in links for c in range(CORES)]


def permute(value, pairs):
    return lax.ppermute(value, AXES, pairs)


def dot(a, b):
    return jnp.dot(a, b, precision=MODE, preferred_element_type=jnp.float32)


def cores_gather(value):
    return lax.all_gather(value, "c", axis=0, tiled=True)


def boundaries(parts, level):
    return range(1 << level, parts, 2 << level)


def upper(p):
    return (p, 0)


def lower(p):
    return (p - 1, CHIPS - 1)


def inverse_pairs(parts, j):
    pairs = []
    for p in range(1, parts):
        for c in range(CORES):
            for chip, base in ((upper(p), 0), (lower(p), CHIPS)):
                r = base + (CHIPS // CORES) * c + j
                pairs.append((flat(p, r // CORES, r % CORES), flat(*chip, c)))
    return pairs


def partner_links(parts, step):
    links = []
    for p in range(step, parts, step):
        links += [(upper(p), lower(p)), (lower(p), upper(p))]
    return links


def cross_links(parts, level):
    s = 1 << level
    links = []
    for p in boundaries(parts, level):
        links += [(upper(p), (p + s - 1, CHIPS - 1)), (lower(p), (p - s, 0))]
    return links


def along_links(parts, level):
    s = 1 << level
    links = []
    for p in boundaries(parts, level):
        if p + s < parts:
            links.append((upper(p), upper(p + s)))
        if p - s > 0:
            links.append((lower(p), lower(p - s)))
    return links


def spread_stages(level):
    s = 1 << level
    last = CHIPS - 1
    stages = []
    steps = [1 << b for b in range(level - 1, -1, -1)]
    if level < 4:
        low, high = {0}, {s - 1}
        for step in steps:
            links = [((d, 0), (d + step, 0)) for d in sorted(low)]
            links += [((d, last), (d - step, last)) for d in sorted(high)]
            low |= {d + step for d in low}
            high |= {d - step for d in high}
            stages.append(links)
    else:
        stages.append([((0, 0), (0, last))])
        low = {0}
        for step in steps:
            stages.append([((d, y), (d + step, y)) for d in sorted(low) for y in (0, last)])
            low |= {d + step for d in low}
    stages.append([((d, a), (d, b)) for d in range(s) for a, b in ((0, 2), (last, last - 2))])
    stages.append(
        [((d, a), (d, b)) for d in range(s) for a, b in ((0, 1), (2, 3), (last, last - 1), (last - 2, last - 3))]
    )
    return stages


def placed(parts, level, links):
    out = []
    for p in boundaries(parts, level):
        for (d, y), (e, w) in links:
            out.append(((p + d, y), (p + e, w)))
            out.append(((p - 1 - d, CHIPS - 1 - y), (p - 1 - e, CHIPS - 1 - w)))
    return out


class Marks:
    def __init__(self, count):
        self.words = [0] * count
        self.bits = 0

    def add(self, links):
        for _, b in links:
            for c in range(CORES):
                self.words[flat(*b, c)] |= 1 << self.bits
        self.bits += 1
        return self.bits - 1


def body(right_side, spikes, inverses):
    parts = lax.axis_size("dom")
    levels, rows, cols = spikes.shape
    me = flat(lax.axis_index("dom"), lax.axis_index("y"), lax.axis_index("c"))
    inverse = inverses[0]

    marks = Marks(parts * CHIPS * CORES)
    trees = []
    for level in range(levels):
        tree = []
        if level < levels - 1:
            links = cross_links(parts, level)
            tree.append((None, marks.add(links)))
        for stage in spread_stages(level):
            links = placed(parts, level, stage)
            tree.append((both_cores(links), marks.add(links)))
        trees.append(tree)
    word = lax.dynamic_index_in_dim(jnp.array(marks.words, jnp.uint32), me, 0, keepdims=False)

    def marked(bit):
        return (word >> bit) & 1 == 1

    b0, b1, t0, t1 = jnp.split(inverse, 4, axis=1)
    for_upper = lax.axis_index("y") < CHIPS // 2
    first, second = jnp.where(for_upper, t0, b0), jnp.where(for_upper, b0, t0)
    third, fourth = jnp.where(for_upper, t1, b1), jnp.where(for_upper, b1, t1)
    arranged = jnp.concatenate([first, second, third, fourth], axis=1)
    own = right_side
    other = permute(own, both_cores(partner_links(parts, 1)))
    pieces = [permute(arranged, inverse_pairs(parts, j)) for j in range(CHIPS // CORES)]
    matrix = jnp.concatenate(pieces, axis=0)
    other_spikes = [
        permute(spikes[level], both_cores(partner_links(parts, 2 << level))) for level in range(levels - 1)
    ]

    out = right_side
    for level in range(levels):
        tips = cores_gather(jnp.concatenate([own, other], axis=0))
        solved = dot(matrix, tips)
        held = solved
        tree = trees[level]
        if level < levels - 1:
            crossed = permute(solved, both_cores(cross_links(parts, level)))
            along = permute(solved, both_cores(along_links(parts, level)))
            own = own - dot(spikes[level], cores_gather(crossed))
            other = other - dot(other_spikes[level], cores_gather(along))
            held = jnp.where(marked(tree[0][1]), crossed, held)
            tree = tree[1:]
        for pairs, bit in tree:
            held = jnp.where(marked(bit), permute(held, pairs), held)
        out = out - dot(spikes[level], cores_gather(held))
    return out


def solution(mesh):
    fine = Mesh(mesh.devices.reshape(mesh.shape["dom"], CHIPS, CORES), AXES)
    rows = ("dom", "y", "c")
    in_specs = (P(rows, None), P(None, rows, None), P("dom", ("y", "c"), None))
    return jax.shard_map(body, mesh=fine, in_specs=in_specs, out_specs=P(rows, None), check_vma=False)
```

time: 866 us -> 220 us (0.25)
  the two profiles are of different devices: /device:TPU:1 before, /device:TPU:13 now
where the time goes in v1:
time: 220 us; the launch traced here: 219 us
  waiting for transfers between devices  97.5 us (44%)
  starting transfers between devices  45.1 us (20%)
  blocking collectives  42 us (19%)
  between operations  18.2 us (8%)
  matrix products  10.1 us (5%)
  local copies, waits for them, and re-layouts  4.6 us (2%)
    ppermute x38, waiting for transfers between devices, permute(): return lax.ppermute(value, AXES, pairs)  97.5 us
    ppermute x38, starting transfers between devices, permute(): return lax.ppermute(value, AXES, pairs)  45.1 us
    all_gather x18, blocking collectives, cores_gather(): return lax.all_gather(value, 'c', axis=0, tiled=True)  42 us
    dot_general x18, matrix products, dot(): return jnp.dot(a, b, precision=MODE, preferred_element_type=jnp.float32)  10.1 us
  transfers between devices with their start and end apart: 38, of which 6 were waited for; matrix products, arithmetic and copies ran while one was open for 6% of the time, Pallas kernels for 0%

profile of v1, /device:TPU:13, one launch (start us, length us, event | category | flops | bytes accessed | tf_op | source)
XLA Modules:
  0.0 219.0 jit_solution(18000801624987039458)
XLA Ops:
  0.0 1.0 copy.7
  1.7 1.0 slice_select_fusion.3
  2.7 0.8 collective-permute-start
  3.5 0.7 collective-permute-start.1
  4.2 0.7 collective-permute-start.2
  4.9 17.0 %collective-permute-start.3 = (f32[64,1024]{1,0:T(8,128)S(1)}, f32[64,1024]{1,0:T(8,128)S(1)}, u32[]{:S(2)}, u32[]{:S(2)}) collective-permute-start(f32[64,1024]{1,0:T(8,128)S(1)} %pad_maximum_fusion), channel_id=1, source_target_pairs={{19,16},{27,14},{23,17},{31,15},{35,32},{43,30},{39,33},{47,31},{5... | collective-permute-start | bytes 786440 | tf_op jit(solution)/shard_map/ppermute | solution.py:21
  22.0 2.2 all_gather.54
  24.3 12.5 %collective-permute-done.3 = f32[64,1024]{1,0:T(8,128)S(1)} collective-permute-done((f32[64,1024]{1,0:T(8,128)S(1)}, f32[64,1024]{1,0:T(8,128)S(1)}, u32[]{:S(2)}, u32[]{:S(2)}) %collective-permute-start.3) | collective-permute-done | bytes 262176 | tf_op jit(solution)/shard_map/ppermute | solution.py:21
  38.1 1.4 slice_bitcast_fusion
  39.5 0.7 collective-permute-start.9
  40.2 0.7 collective-permute-start.15
  40.9 0.7 collective-permute-start.22
  41.6 0.7 collective-permute-start.30
  42.3 1.4 dynamic_slice.4
  61.6 2.0 all_gather.56
  64.3 2.0 all_gather.57
  66.3 1.4 fusion.7
  67.7 1.4 fusion.6
  69.2 2.2 all_gather.58
  72.7 0.7 collective-permute-start.10
  73.4 1.3 collective-permute-start.7
  74.7 2.0 all_gather.61
  76.7 2.0 all_gather.60
  79.5 2.2 all_gather.62
  82.3 0.7 collective-permute-start.21
  82.9 0.7 collective-permute-start.16
  83.6 38.5 %collective-permute-done.7 = f32[256,128]{1,0:T(8,128)S(1)} collective-permute-done((f32[256,128]{1,0:T(8,128)S(1)}, f32[256,128]{1,0:T(8,128)S(1)}, u32[]{:S(2)}, u32[]{:S(2)}) %collective-permute-start.7) | collective-permute-done | bytes 131104 | tf_op jit(solution)/shard_map/ppermute | solution.py:21
  122.8 3.7 %all_gather.55 = f32[512,128]{1,0:T(8,128)S(1)} all-gather(f32[256,128]{1,0:T(8,128)S(1)} %broadcast_select_fusion.24), channel_id=1, replica_groups=mesh['dom'=32,'y'=8,'c'=2] {'c'}, dimensions={0}, use_global_device_ids=true | all-gather | bytes 393216 | tf_op jit(solution)/shard_map/all_gather | solution.py:29
  126.5 2.0 all_gather.65
  128.5 2.0 all_gather.64
  131.3 2.2 all_gather.66
  136.2 0.7 collective-permute-start.12
  136.9 2.0 all_gather.69
  138.9 2.0 all_gather.68
  141.7 2.2 all_gather.70
  146.6 1.3 collective-permute-start.13
  150.0 24.4 %collective-permute-done.13 = f32[256,128]{1,0:T(8,128)S(1)} collective-permute-done((f32[256,128]{1,0:T(8,128)S(1)}, f32[256,128]{1,0:T(8,128)S(1)}, u32[]{:S(2)}, u32[]{:S(2)}) %collective-permute-start.13) | collective-permute-done | bytes 131104 | tf_op jit(solution)/shard_map/ppermute | solution.py:21
  174.5 2.6 %all_gather.59 = f32[512,128]{1,0:T(8,128)S(1)} all-gather(f32[256,128]{1,0:T(8,128)S(1)} %broadcast_select_fusion.21), channel_id=1, replica_groups=mesh['dom'=32,'y'=8,'c'=2] {'c'}, dimensions={0}, use_global_device_ids=true | all-gather | bytes 393216 | tf_op jit(solution)/shard_map/all_gather | solution.py:29
  178.9 1.3 collective-permute-start.20
  181.7 9.6 %collective-permute-done.20 = f32[256,128]{1,0:T(8,128)S(1)} collective-permute-done((f32[256,128]{1,0:T(8,128)S(1)}, f32[256,128]{1,0:T(8,128)S(1)}, u32[]{:S(2)}, u32[]{:S(2)}) %collective-permute-start.20) | collective-permute-done | bytes 131104 | tf_op jit(solution)/shard_map/ppermute | solution.py:21
  191.3 2.9 %all_gather.63 = f32[512,128]{1,0:T(8,128)S(1)} all-gather(f32[256,128]{1,0:T(8,128)S(1)} %broadcast_select_fusion.17), channel_id=1, replica_groups=mesh['dom'=32,'y'=8,'c'=2] {'c'}, dimensions={0}, use_global_device_ids=true | all-gather | bytes 393216 | tf_op jit(solution)/shard_map/all_gather | solution.py:29
  195.2 1.3 collective-permute-start.28
  197.3 7.5 %collective-permute-done.28 = f32[256,128]{1,0:T(8,128)S(1)} collective-permute-done((f32[256,128]{1,0:T(8,128)S(1)}, f32[256,128]{1,0:T(8,128)S(1)}, u32[]{:S(2)}, u32[]{:S(2)}) %collective-permute-start.28) | collective-permute-done | bytes 131104 | tf_op jit(solution)/shard_map/ppermute | solution.py:21
  204.8 3.2 %all_gather.67 = f32[512,128]{1,0:T(8,128)S(1)} all-gather(f32[256,128]{1,0:T(8,128)S(1)} %broadcast_select_fusion.12), channel_id=1, replica_groups=mesh['dom'=32,'y'=8,'c'=2] {'c'}, dimensions={0}, use_global_device_ids=true | all-gather | bytes 393216 | tf_op jit(solution)/shard_map/all_gather | solution.py:29
  208.0 1.3 collective-permute-start.37
  209.7 4.9 %collective-permute-done.37 = f32[256,128]{1,0:T(8,128)S(1)} collective-permute-done((f32[256,128]{1,0:T(8,128)S(1)}, f32[256,128]{1,0:T(8,128)S(1)}, u32[]{:S(2)}, u32[]{:S(2)}) %collective-permute-start.37) | collective-permute-done | bytes 131104 | tf_op jit(solution)/shard_map/ppermute | solution.py:21
  214.6 2.9 %all_gather.71 = f32[512,128]{1,0:T(8,128)S(1)} all-gather(f32[256,128]{1,0:T(8,128)S(1)} %broadcast_select_fusion.6), channel_id=1, replica_groups=mesh['dom'=32,'y'=8,'c'=2] {'c'}, dimensions={0}, use_global_device_ids=true | all-gather | bytes 393216 | tf_op jit(solution)/shard_map/all_gather | solution.py:29
  218.2 0.8 copy.9
  (110 shorter events, 21.9 us)
Async XLA Ops:
  1.0 20.9 %collective-permute-start.4 = (f32[256,128]{0,1:T(8,128)S(1)}, f32[256,128]{0,1:T(8,128)S(1)}, u32[]{:S(2)}, u32[]{:S(2)}) collective-permute-start(f32[256,128]{0,1:T(8,128)S(1)} %copy.7), channel_id=1, source_target_pairs={{16,14},{17,15},{14,16},{15,17},{32,30},{33,31},{30,32},{31,33},{4... | collective-permute-start | bytes 393224 | tf_op jit(solution)/shard_map/ppermute | solution.py:21
  2.7 35.4 %copy-start = (f32[5,256,512]{2,1,0:T(8,128)S(1)}, f32[5,256,512]{2,1,0:T(8,128)}, u32[]{:S(2)}) copy-start(f32[5,256,512]{2,1,0:T(8,128)} %param.5) | copy-start | bytes 7864324
  2.7 21.5 %collective-permute-start = (f32[64,1024]{1,0:T(8,128)S(1)}, f32[64,1024]{1,0:T(8,128)S(1)}, u32[]{:S(2)}, u32[]{:S(2)}) collective-permute-start(f32[64,1024]{1,0:T(8,128)S(1)} %pad_maximum_fusion), channel_id=1, source_target_pairs={{16,16},{24,14},{20,17},{28,15},{32,32},{40,30},{36,33},{44,31},{4... | collective-permute-start | bytes 786440 | tf_op jit(solution)/shard_map/ppermute | solution.py:21
  3.5 20.7 %collective-permute-start.1 = (f32[64,1024]{1,0:T(8,128)S(1)}, f32[64,1024]{1,0:T(8,128)S(1)}, u32[]{:S(2)}, u32[]{:S(2)}) collective-permute-start(f32[64,1024]{1,0:T(8,128)S(1)} %pad_maximum_fusion), channel_id=1, source_target_pairs={{17,16},{25,14},{21,17},{29,15},{33,32},{41,30},{37,33},{45,31},{4... | collective-permute-start | bytes 786440 | tf_op jit(solution)/shard_map/ppermute | solution.py:21
  4.2 20.0 %collective-permute-start.2 = (f32[64,1024]{1,0:T(8,128)S(1)}, f32[64,1024]{1,0:T(8,128)S(1)}, u32[]{:S(2)}, u32[]{:S(2)}) collective-permute-start(f32[64,1024]{1,0:T(8,128)S(1)} %pad_maximum_fusion), channel_id=1, source_target_pairs={{18,16},{26,14},{22,17},{30,15},{34,32},{42,30},{38,33},{46,31},{5... | collective-permute-start | bytes 786440 | tf_op jit(solution)/shard_map/ppermute | solution.py:21
  4.9 31.9 %collective-permute-start.3 = (f32[64,1024]{1,0:T(8,128)S(1)}, f32[64,1024]{1,0:T(8,128)S(1)}, u32[]{:S(2)}, u32[]{:S(2)}) collective-permute-start(f32[64,1024]{1,0:T(8,128)S(1)} %pad_maximum_fusion), channel_id=1, source_target_pairs={{19,16},{27,14},{23,17},{31,15},{35,32},{43,30},{39,33},{47,31},{5... | collective-permute-start | bytes 786440 | tf_op jit(solution)/shard_map/ppermute | solution.py:21
  21.9 2.2 %copy-start.2 = (f32[256,128]{0,1:T(8,128)}, f32[256,128]{0,1:T(8,128)S(1)}, u32[]{:S(2)}) copy-start(f32[256,128]{0,1:T(8,128)S(1)} %collective-permute-done.4) | copy-start | bytes 393220
  37.4 23.5 %collective-permute-start.5 = (f32[256,128]{1,0:T(8,128)S(1)}, f32[256,128]{1,0:T(8,128)S(1)}, u32[]{:S(2)}, u32[]{:S(2)}) collective-permute-start(f32[256,128]{1,0:T(8,128)S(1)} %fusion.15), channel_id=1, source_target_pairs={{16,30},{17,31},{14,0},{15,1},{48,62},{49,63},{46,32},{47,33},{80,... | collective-permute-start | bytes 393224 | tf_op jit(solution)/shard_map/ppermute | solution.py:21
  39.5 28.2 %collective-permute-start.9 = (f32[256,512]{1,0:T(8,128)}, f32[256,512]{1,0:T(8,128)S(1)}, u32[]{:S(2)}, u32[]{:S(2)}) collective-permute-start(f32[256,512]{1,0:T(8,128)} %get-tuple-element.8), channel_id=1, source_target_pairs={{32,30},{33,31},{30,32},{31,33},{64,62},{65,63},{62,64},{63,65},{9... | collective-permute-start | bytes 1572872 | tf_op jit(solution)/shard_map/ppermute | solution.py:21
  40.2 38.9 %collective-permute-start.15 = (f32[256,512]{1,0:T(8,128)}, f32[256,512]{1,0:T(8,128)S(1)}, u32[]{:S(2)}, u32[]{:S(2)}) collective-permute-start(f32[256,512]{1,0:T(8,128)} %get-tuple-element.7), channel_id=1, source_target_pairs={{64,62},{65,63},{62,64},{63,65},{128,126},{129,127},{126,128},{127... | collective-permute-start | bytes 1572872 | tf_op jit(solution)/shard_map/ppermute | solution.py:21
  40.9 90.0 %collective-permute-start.22 = (f32[256,512]{1,0:T(8,128)}, f32[256,512]{1,0:T(8,128)S(1)}, u32[]{:S(2)}, u32[]{:S(2)}) collective-permute-start(f32[256,512]{1,0:T(8,128)} %get-tuple-element.6), channel_id=1, source_target_pairs={{128,126},{129,127},{126,128},{127,129},{256,254},{257,255},{254,2... | collective-permute-start | bytes 1572872 | tf_op jit(solution)/shard_map/ppermute | solution.py:21
  41.6 99.7 %collective-permute-start.30 = (f32[256,512]{1,0:T(8,128)}, f32[256,512]{1,0:T(8,128)S(1)}, u32[]{:S(2)}, u32[]{:S(2)}) collective-permute-start(f32[256,512]{1,0:T(8,128)} %get-tuple-element.5), channel_id=1, source_target_pairs={{256,254},{257,255},{254,256},{255,257}} | collective-permute-start | bytes 1572872 | tf_op jit(solution)/shard_map/ppermute | solution.py:21
  60.9 2.7 %collective-permute-start.8 = (f32[256,128]{1,0:T(8,128)S(1)}, f32[256,128]{1,0:T(8,128)S(1)}, u32[]{:S(2)}, u32[]{:S(2)}) collective-permute-start(f32[256,128]{1,0:T(8,128)S(1)} %fusion.15), channel_id=1, source_target_pairs={{16,32},{17,33},{48,64},{49,65},{46,30},{47,31},{80,96},{81,97},{7... | collective-permute-start | bytes 393224 | tf_op jit(solution)/shard_map/ppermute | solution.py:21
  63.6 9.1 %collective-permute-start.6 = (f32[256,128]{1,0:T(8,128)S(1)}, f32[256,128]{1,0:T(8,128)S(1)}, u32[]{:S(2)}, u32[]{:S(2)}) collective-permute-start(f32[256,128]{1,0:T(8,128)S(1)} %broadcast_select_fusion.22), channel_id=1, source_target_pairs={{16,20},{17,21},{14,10},{15,11},{30,26},{31,27},{0,4},{1,5},{48,52... | collective-permute-start | bytes 393224 | tf_op jit(solution)/shard_map/ppermute | solution.py:21
  67.7 11.0 %copy-start.1 = (f32[5,256,512]{2,1,0:T(8,128)S(1)}, f32[5,256,512]{2,1,0:T(8,128)}, u32[]{:S(2)}) copy-start(f32[5,256,512]{2,1,0:T(8,128)} %param.5) | copy-start | bytes 7864324
  72.0 1.4 collective-permute-start.14
  72.7 4.0 %collective-permute-start.10 = (f32[256,128]{1,0:T(8,128)S(1)}, f32[256,128]{1,0:T(8,128)S(1)}, u32[]{:S(2)}, u32[]{:S(2)}) collective-permute-start(f32[256,128]{1,0:T(8,128)S(1)} %fusion.16), channel_id=1, source_target_pairs={{32,62},{33,63},{30,0},{31,1},{96,126},{97,127},{94,64},{95,65},{1... | collective-permute-start | bytes 393224 | tf_op jit(solution)/shard_map/ppermute | solution.py:21
  73.4 48.8 %collective-permute-start.7 = (f32[256,128]{1,0:T(8,128)S(1)}, f32[256,128]{1,0:T(8,128)S(1)}, u32[]{:S(2)}, u32[]{:S(2)}) collective-permute-start(f32[256,128]{1,0:T(8,128)S(1)} %broadcast_select_fusion.23), channel_id=1, source_target_pairs={{16,18},{17,19},{14,12},{15,13},{20,22},{21,23},{10,8},{11,9},{30,... | collective-permute-start | bytes 393224 | tf_op jit(solution)/shard_map/ppermute | solution.py:21
  82.3 44.3 %collective-permute-start.21 = (f32[256,128]{1,0:T(8,128)S(1)}, f32[256,128]{1,0:T(8,128)S(1)}, u32[]{:S(2)}, u32[]{:S(2)}) collective-permute-start(f32[256,128]{1,0:T(8,128)S(1)} %fusion.17), channel_id=1, source_target_pairs={{64,128},{65,129},{192,256},{193,257},{190,126},{191,127},{320,384... | collective-permute-start | bytes 393224 | tf_op jit(solution)/shard_map/ppermute | solution.py:21
  82.9 45.6 %collective-permute-start.16 = (f32[256,128]{1,0:T(8,128)S(1)}, f32[256,128]{1,0:T(8,128)S(1)}, u32[]{:S(2)}, u32[]{:S(2)}) collective-permute-start(f32[256,128]{1,0:T(8,128)S(1)} %fusion.17), channel_id=1, source_target_pairs={{64,126},{65,127},{62,0},{63,1},{192,254},{193,255},{190,128},{191... | collective-permute-start | bytes 393224 | tf_op jit(solution)/shard_map/ppermute | solution.py:21
  122.1 14.0 %collective-permute-start.11 = (f32[256,128]{1,0:T(8,128)S(1)}, f32[256,128]{1,0:T(8,128)S(1)}, u32[]{:S(2)}, u32[]{:S(2)}) collective-permute-start(f32[256,128]{1,0:T(8,128)S(1)} %broadcast_select_fusion.18), channel_id=1, source_target_pairs={{32,48},{33,49},{30,14},{31,15},{62,46},{63,47},{0,16},{1,17},{96,... | collective-permute-start | bytes 393224 | tf_op jit(solution)/shard_map/ppermute | solution.py:21
  134.1 2.8 %collective-permute-start.29 = (f32[256,128]{1,0:T(8,128)S(1)}, f32[256,128]{1,0:T(8,128)S(1)}, u32[]{:S(2)}, u32[]{:S(2)}) collective-permute-start(f32[256,128]{1,0:T(8,128)S(1)} %fusion.18), channel_id=1, source_target_pairs={{128,256},{129,257},{382,254},{383,255}} | collective-permute-start | bytes 393224 | tf_op jit(solution)/shard_map/ppermute | solution.py:21
  134.8 4.1 %collective-permute-start.23 = (f32[256,128]{1,0:T(8,128)S(1)}, f32[256,128]{1,0:T(8,128)S(1)}, u32[]{:S(2)}, u32[]{:S(2)}) collective-permute-start(f32[256,128]{1,0:T(8,128)S(1)} %fusion.18), channel_id=1, source_target_pairs={{128,254},{129,255},{126,0},{127,1},{384,510},{385,511},{382,256},... | collective-permute-start | bytes 393224 | tf_op jit(solution)/shard_map/ppermute | solution.py:21
  135.5 10.4 %collective-permute-start.17 = (f32[256,128]{1,0:T(8,128)S(1)}, f32[256,128]{1,0:T(8,128)S(1)}, u32[]{:S(2)}, u32[]{:S(2)}) collective-permute-start(f32[256,128]{1,0:T(8,128)S(1)} %broadcast_select_fusion.13), channel_id=1, source_target_pairs={{64,96},{65,97},{62,30},{63,31},{126,94},{127,95},{0,32},{1,33},{1... | collective-permute-start | bytes 393224 | tf_op jit(solution)/shard_map/ppermute | solution.py:21
  136.2 10.4 %collective-permute-start.12 = (f32[256,128]{1,0:T(8,128)S(1)}, f32[256,128]{1,0:T(8,128)S(1)}, u32[]{:S(2)}, u32[]{:S(2)}) collective-permute-start(f32[256,128]{1,0:T(8,128)S(1)} %broadcast_select_fusion.19), channel_id=1, source_target_pairs={{32,36},{33,37},{30,26},{31,27},{46,42},{47,43},{16,20},{17,21},{4... | collective-permute-start | bytes 393224 | tf_op jit(solution)/shard_map/ppermute | solution.py:21
  144.5 3.4 %collective-permute-start.31 = (f32[256,128]{1,0:T(8,128)S(1)}, f32[256,128]{1,0:T(8,128)S(1)}, u32[]{:S(2)}, u32[]{:S(2)}) collective-permute-start(f32[256,128]{1,0:T(8,128)S(1)} %fusion.19), channel_id=1, source_target_pairs={{256,270},{257,271},{254,240},{255,241}} | collective-permute-start | bytes 393224 | tf_op jit(solution)/shard_map/ppermute | solution.py:21
  145.2 3.4 %collective-permute-start.24 = (f32[256,128]{1,0:T(8,128)S(1)}, f32[256,128]{1,0:T(8,128)S(1)}, u32[]{:S(2)}, u32[]{:S(2)}) collective-permute-start(f32[256,128]{1,0:T(8,128)S(1)} %broadcast_select_fusion.7), channel_id=1, source_target_pairs={{128,192},{129,193},{126,62},{127,63},{254,190},{255,191},{0,64},{... | collective-permute-start | bytes 393224 | tf_op jit(solution)/shard_map/ppermute | solution.py:21
  145.9 3.4 %collective-permute-start.18 = (f32[256,128]{1,0:T(8,128)S(1)}, f32[256,128]{1,0:T(8,128)S(1)}, u32[]{:S(2)}, u32[]{:S(2)}) collective-permute-start(f32[256,128]{1,0:T(8,128)S(1)} %broadcast_select_fusion.14), channel_id=1, source_target_pairs={{64,80},{65,81},{62,46},{63,47},{96,112},{97,113},{30,14},{31,15},... | collective-permute-start | bytes 393224 | tf_op jit(solution)/shard_map/ppermute | solution.py:21
  146.6 27.9 %collective-permute-start.13 = (f32[256,128]{1,0:T(8,128)S(1)}, f32[256,128]{1,0:T(8,128)S(1)}, u32[]{:S(2)}, u32[]{:S(2)}) collective-permute-start(f32[256,128]{1,0:T(8,128)S(1)} %broadcast_select_fusion.20), channel_id=1, source_target_pairs={{32,34},{33,35},{30,28},{31,29},{36,38},{37,39},{26,24},{27,25},{4... | collective-permute-start | bytes 393224 | tf_op jit(solution)/shard_map/ppermute | solution.py:21
  147.9 29.5 %collective-permute-start.32 = (f32[256,128]{1,0:T(8,128)S(1)}, f32[256,128]{1,0:T(8,128)S(1)}, u32[]{:S(2)}, u32[]{:S(2)}) collective-permute-start(f32[256,128]{1,0:T(8,128)S(1)} %broadcast_select_fusion), channel_id=1, source_target_pairs={{256,384},{257,385},{254,126},{255,127},{270,398},{271,399},{240,1... | collective-permute-start | bytes 393224 | tf_op jit(solution)/shard_map/ppermute | solution.py:21
  148.7 29.5 %collective-permute-start.25 = (f32[256,128]{1,0:T(8,128)S(1)}, f32[256,128]{1,0:T(8,128)S(1)}, u32[]{:S(2)}, u32[]{:S(2)}) collective-permute-start(f32[256,128]{1,0:T(8,128)S(1)} %broadcast_select_fusion.8), channel_id=1, source_target_pairs={{128,160},{129,161},{126,94},{127,95},{192,224},{193,225},{62,30},... | collective-permute-start | bytes 393224 | tf_op jit(solution)/shard_map/ppermute | solution.py:21
  149.4 29.5 %collective-permute-start.19 = (f32[256,128]{1,0:T(8,128)S(1)}, f32[256,128]{1,0:T(8,128)S(1)}, u32[]{:S(2)}, u32[]{:S(2)}) collective-permute-start(f32[256,128]{1,0:T(8,128)S(1)} %broadcast_select_fusion.15), channel_id=1, source_target_pairs={{64,68},{65,69},{62,58},{63,59},{78,74},{79,75},{48,52},{49,53},{8... | collective-permute-start | bytes 393224 | tf_op jit(solution)/shard_map/ppermute | solution.py:21
  177.5 2.7 %collective-permute-start.33 = (f32[256,128]{1,0:T(8,128)S(1)}, f32[256,128]{1,0:T(8,128)S(1)}, u32[]{:S(2)}, u32[]{:S(2)}) collective-permute-start(f32[256,128]{1,0:T(8,128)S(1)} %broadcast_select_fusion.1), channel_id=1, source_target_pairs={{256,320},{257,321},{254,190},{255,191},{270,334},{271,335},{240,1... | collective-permute-start | bytes 393224 | tf_op jit(solution)/shard_map/ppermute | solution.py:21
  178.2 2.7 %collective-permute-start.26 = (f32[256,128]{1,0:T(8,128)S(1)}, f32[256,128]{1,0:T(8,128)S(1)}, u32[]{:S(2)}, u32[]{:S(2)}) collective-permute-start(f32[256,128]{1,0:T(8,128)S(1)} %broadcast_select_fusion.9), channel_id=1, source_target_pairs={{128,144},{129,145},{126,110},{127,111},{160,176},{161,177},{94,78... | collective-permute-start | bytes 393224 | tf_op jit(solution)/shard_map/ppermute | solution.py:21
  178.9 12.3 %collective-permute-start.20 = (f32[256,128]{1,0:T(8,128)S(1)}, f32[256,128]{1,0:T(8,128)S(1)}, u32[]{:S(2)}, u32[]{:S(2)}) collective-permute-start(f32[256,128]{1,0:T(8,128)S(1)} %broadcast_select_fusion.16), channel_id=1, source_target_pairs={{64,66},{65,67},{62,60},{63,61},{68,70},{69,71},{58,56},{59,57},{7... | collective-permute-start | bytes 393224 | tf_op jit(solution)/shard_map/ppermute | solution.py:21
  180.3 14.2 %collective-permute-start.34 = (f32[256,128]{1,0:T(8,128)S(1)}, f32[256,128]{1,0:T(8,128)S(1)}, u32[]{:S(2)}, u32[]{:S(2)}) collective-permute-start(f32[256,128]{1,0:T(8,128)S(1)} %broadcast_select_fusion.2), channel_id=1, source_target_pairs={{256,288},{257,289},{254,222},{255,223},{270,302},{271,303},{240,2... | collective-permute-start | bytes 393224 | tf_op jit(solution)/shard_map/ppermute | solution.py:21
  181.0 14.2 %collective-permute-start.27 = (f32[256,128]{1,0:T(8,128)S(1)}, f32[256,128]{1,0:T(8,128)S(1)}, u32[]{:S(2)}, u32[]{:S(2)}) collective-permute-start(f32[256,128]{1,0:T(8,128)S(1)} %broadcast_select_fusion.10), channel_id=1, source_target_pairs={{128,132},{129,133},{126,122},{127,123},{142,138},{143,139},{112,1... | collective-permute-start | bytes 393224 | tf_op jit(solution)/shard_map/ppermute | solution.py:21
  194.5 2.0 collective-permute-start.35
  195.2 9.5 %collective-permute-start.28 = (f32[256,128]{1,0:T(8,128)S(1)}, f32[256,128]{1,0:T(8,128)S(1)}, u32[]{:S(2)}, u32[]{:S(2)}) collective-permute-start(f32[256,128]{1,0:T(8,128)S(1)} %broadcast_select_fusion.11), channel_id=1, source_target_pairs={{128,130},{129,131},{126,124},{127,125},{132,134},{133,135},{122,1... | collective-permute-start | bytes 393224 | tf_op jit(solution)/shard_map/ppermute | solution.py:21
  196.6 11.4 %collective-permute-start.36 = (f32[256,128]{1,0:T(8,128)S(1)}, f32[256,128]{1,0:T(8,128)S(1)}, u32[]{:S(2)}, u32[]{:S(2)}) collective-permute-start(f32[256,128]{1,0:T(8,128)S(1)} %broadcast_select_fusion.4), channel_id=1, source_target_pairs={{256,260},{257,261},{254,250},{255,251},{270,266},{271,267},{240,2... | collective-permute-start | bytes 393224 | tf_op jit(solution)/shard_map/ppermute | solution.py:21
  208.0 6.6 %collective-permute-start.37 = (f32[256,128]{1,0:T(8,128)S(1)}, f32[256,128]{1,0:T(8,128)S(1)}, u32[]{:S(2)}, u32[]{:S(2)}) collective-permute-start(f32[256,128]{1,0:T(8,128)S(1)} %broadcast_select_fusion.5), channel_id=1, source_target_pairs={{256,258},{257,259},{254,252},{255,253},{260,262},{261,263},{250,2... | collective-permute-start | bytes 393224 | tf_op jit(solution)/shard_map/ppermute | solution.py:21

commit v2 on v0

v2 whole, which is shorter than its diff:
```python
import jax
import jax.numpy as jnp
from jax import lax
from jax.sharding import Mesh
from jax.sharding import PartitionSpec as P


CHIPS, CORES, RING = 8, 2, 8
LAST = CHIPS - 1
AXES = ("dom", "y", "c")
MODE = lax.Precision.HIGH


def flat(dom, y, c):
    return (dom * CHIPS + y) * CORES + c


def both_cores(links):
    return [(flat(*a, c), flat(*b, c)) for a, b in links for c in range(CORES)]


def permute(value, links):
    return lax.ppermute(value, AXES, both_cores(links))


def swap_cores(value):
    return lax.ppermute(value, "c", [(0, 1), (1, 0)])


def cores_gather(value):
    return lax.all_gather(value, "c", axis=0, tiled=True)


def dot_t(a, b):
    return lax.dot_general(a, b, (((1,), (1,)), ((), ())), precision=MODE, preferred_element_type=jnp.float32)


def boundaries(parts, level):
    return range(1 << level, parts, 2 << level)


def upper(p):
    return (p, 0)


def lower(p):
    return (p - 1, LAST)


def inverse_links(parts, j):
    links = []
    for p in range(1, parts):
        links += [((p, j), upper(p)), ((p, (j + CHIPS // 2) % CHIPS), lower(p))]
    return links


def cross_links(parts, level):
    s = 1 << level
    links = []
    for p in boundaries(parts, level):
        links += [(upper(p), (p + s - 1, LAST)), (lower(p), (p - s, 0))]
    return links


def along_links(parts, level):
    s = 1 << level
    links = []
    for p in boundaries(parts, level):
        links += [(upper(p), (p - s, 0)), (lower(p), (p + s - 1, LAST))]
    return links


def partner_links(parts, step):
    links = []
    for p in range(step, parts, step):
        links += [(upper(p), lower(p)), (lower(p), upper(p))]
    return links


def corner_links(parts, bit):
    step = 1 << bit
    low = 2 * step - 1
    links = []
    for q in range(parts):
        if q & low == low:
            links.append(((q, LAST), (q - step, LAST)))
        if q & low == 0:
            links.append(((q, 0), (q + step, 0)))
    return links


def top_links(parts, moves):
    p = parts // 2
    links = []
    for a, b in moves:
        links += [((p + a, 0), (p + b, 0)), ((p - 1 - a, LAST), (p - 1 - b, LAST))]
    return links


def chip_links(parts, pairs):
    return [((q, a), (q, b)) for q in range(parts) for a, b in pairs]


ENDS = ((0, LAST), (LAST, 0))
INNER = ((0, 2), (LAST, LAST - 2))
REST = ((0, 1), (2, 3), (LAST, LAST - 1), (LAST - 2, LAST - 3))


def body(right_side, spikes, inverses):
    parts = lax.axis_size("dom")
    levels, _, cols = spikes.shape
    top = levels - 1
    first_core = lax.axis_index("c") == 0
    mine = lax.axis_index("c") * (right_side.shape[1] // CORES)

    inverse = inverses[0]
    below, above = inverse[:, :cols], inverse[:, cols:]
    for_upper = lax.axis_index("y") < CHIPS // 2
    sent = jnp.where(for_upper, above, below), jnp.where(for_upper, below, above)
    pieces = [permute(sent[j // (CHIPS // 2)], inverse_links(parts, j)) for j in range(CHIPS)]
    blocks = []
    for j in range(0, CHIPS, 2):
        gathered = cores_gather(jnp.concatenate(pieces[j : j + 2], axis=0))
        blocks += [jnp.split(gathered, 4, axis=0)[i] for i in (0, 2, 1, 3)]
    stay, go = jnp.concatenate(blocks[:CHIPS], axis=0), jnp.concatenate(blocks[CHIPS:], axis=0)

    both = cores_gather(right_side)
    own = lax.dynamic_slice_in_dim(both.T, mine, right_side.shape[1] // CORES, 0)
    here, there = spikes, swap_cores(spikes)
    tip_spikes = [
        jnp.concatenate(
            [jnp.where(first_core, here[k], there[k]), jnp.where(first_core, there[k], here[k])], axis=0
        )
        for k in range(top)
    ]

    held = []
    for level in range(levels):
        near = dot_t(own, stay)
        if level == top:
            far = dot_t(own, go)
            break
        solved = permute(near, cross_links(parts, level))
        far = dot_t(own, go)
        solved = solved + permute(far, along_links(parts, level))
        own = own - dot_t(solved, tip_spikes[level])
        held.append(solved)

    def spread_chips(value):
        for pairs in (ENDS, INNER, REST):
            value = value + permute(value, chip_links(parts, pairs))
        return value

    width = solved.shape[0]
    moved = held[1] + permute(held[1], corner_links(parts, 0))
    low = spread_chips(jnp.concatenate([held[0], moved], axis=0))
    third = held[3] + permute(held[3], corner_links(parts, 2))
    third = jnp.concatenate([held[2], third], axis=0)
    for bit in (1, 0):
        third = third + permute(third, corner_links(parts, bit))

    p = parts // 2
    at_root = (lax.axis_index("y") == 0) & (lax.axis_index("dom") == p)
    at_root |= (lax.axis_index("y") == LAST) & (lax.axis_index("dom") == p - 1)
    solved = jnp.where(at_root, near, 0.0) + permute(far, partner_links(parts, p))
    last = solved + permute(solved, top_links(parts, [(0, RING)]))
    lines = range(0, p, RING)
    for k, (starts, ends) in enumerate(((((0, 3), (0, 5)), ()), (((0, 1), (3, 4), (5, 6)), ((0, 7), (3, 2))))):
        if k == 0:
            sets = [[starts[0]], [starts[1]]]
        else:
            sets = [starts, ends]
        got = [permute(last, top_links(parts, [(n + a, n + b) for n in lines for a, b in moves])) for moves in sets]
        last = last + got[0] + got[1]
    pair = spread_chips(jnp.concatenate([third, last], axis=0))

    def spread_update(out, level, full):
        return out - lax.dot_general(
            spikes[level], full, (((1,), (1,)), ((), ())), precision=MODE, preferred_element_type=jnp.float32
        )

    out = right_side
    for value, first in ((low, 0), (pair, 2)):
        count = value.shape[0] // width
        ends = cores_gather(value)
        for k in range(count):
            full = jnp.concatenate([ends[i * width : (i + 1) * width] for i in (k, k + count)], axis=0)
            out = spread_update(out, first + k, full)
    return out


def solution(mesh):
    fine = Mesh(mesh.devices.reshape(mesh.shape["dom"], CHIPS, CORES), AXES)
    rows = ("dom", "y", "c")
    in_specs = (P(rows, None), P(None, rows, None), P("dom", ("y", "c"), None))

    return jax.shard_map(body, mesh=fine, in_specs=in_specs, out_specs=P(rows, None), check_vma=False)
```

time: 866 us -> 175 us (0.20)
  the two profiles are of different devices: /device:TPU:1 before, /device:TPU:159 now
where the time goes in v2:
time: 175 us
  waiting for transfers between devices  88.2 us (50%)
  blocking collectives  36.3 us (21%)
  starting transfers between devices  31.8 us (18%)
  matrix products  10.7 us (6%)
  other arithmetic  4.67 us (3%)
  local copies, waits for them, and re-layouts  2.05 us (1%)
    ppermute x32, waiting for transfers between devices, permute(): return lax.ppermute(value, AXES, both_cores(links))  88.2 us
    all_gather x7, blocking collectives, cores_gather(): return lax.all_gather(value, 'c', axis=0, tiled=True)  36.3 us
    ppermute x32, starting transfers between devices, permute(): return lax.ppermute(value, AXES, both_cores(links))  29.5 us
    dot_general x14, matrix products, dot_t(): lax.dot_general(a, b, (((1,), (1,)), ((), ())), precision=MODE, preferred...  8.58 us
  transfers between devices with their start and end apart: 33, of which 2 were waited for; matrix products, arithmetic and copies ran while one was open for 3% of the time, Pallas kernels for 0%

profile of v2, /device:TPU:159, one launch (start us, length us, event | category | flops | bytes accessed | tf_op | source)
XLA Modules:
  0.0 174.6 jit_solution(7388626262020114144)
XLA Ops:
  0.0 1.0 slice_select_fusion
  1.0 0.7 collective-permute-start.6
  1.7 0.7 collective-permute-start.5
  2.3 5.1 %collective-permute-start.8 = (f32[64,512]{1,0:T(8,128)S(1)}, f32[64,512]{1,0:T(8,128)S(1)}, u32[]{:S(2)}, u32[]{:S(2)}) collective-permute-start(f32[64,512]{1,0:T(8,128)S(1)} %get-tuple-element.23), channel_id=1, source_target_pairs={{30,16},{31,17},{22,14},{23,15},{46,32},{47,33},{38,30},{39,31},{6... | collective-permute-start | bytes 393224 | tf_op jit(solution)/shard_map/ppermute | solution.py:23
  7.4 0.7 collective-permute-start.7
  8.1 2.8 %collective-permute-start.3 = (f32[64,512]{1,0:T(8,128)S(1)}, f32[64,512]{1,0:T(8,128)S(1)}, u32[]{:S(2)}, u32[]{:S(2)}) collective-permute-start(f32[64,512]{1,0:T(8,128)S(1)} %get-tuple-element.24), channel_id=1, source_target_pairs={{22,16},{23,17},{30,14},{31,15},{38,32},{39,33},{46,30},{47,31},{5... | collective-permute-start | bytes 393224 | tf_op jit(solution)/shard_map/ppermute | solution.py:23
  11.0 1.0 copy.5
  12.0 2.9 %all_gather.21 = f32[512,128]{0,1:T(8,128)S(1)} all-gather(f32[256,128]{0,1:T(8,128)S(1)} %copy.5), channel_id=1, replica_groups=mesh['dom'=32,'y'=8,'c'=2] {'c'}, dimensions={0}, use_global_device_ids=true | all-gather | bytes 393216 | tf_op jit(solution)/shard_map/all_gather | solution.py:31
  14.8 0.7 collective-permute-start.2
  15.5 0.7 collective-permute-start.1
  16.2 2.2 %all_gather.24 = f32[256,512]{1,0:T(8,128)S(1)} all-gather(f32[128,512]{1,0:T(8,128)S(1)} %pad_maximum_fusion.3), channel_id=1, replica_groups=mesh['dom'=32,'y'=8,'c'=2] {'c'}, dimensions={0}, use_global_device_ids=true | all-gather | bytes 786432 | tf_op jit(solution)/shard_map/all_gather | solution.py:31
  18.4 0.7 collective-permute-start
  19.1 2.3 %collective-permute-start.10 = (f32[5,256,512]{2,1,0:T(8,128)}, f32[5,256,512]{2,1,0:T(8,128)}, u32[]{:S(2)}, u32[]{:S(2)}) collective-permute-start(f32[5,256,512]{2,1,0:T(8,128)} %param.4), channel_id=1, source_target_pairs={{0,1},{1,0},{2,3},{3,2},{4,5},{5,4},{6,7},{7,6},{8,9},{9,8},{10,11... | collective-permute-start | bytes 7864328 | tf_op jit(solution)/shard_map/ppermute | solution.py:27
  21.4 5.1 %all_gather.25 = f32[256,512]{1,0:T(8,128)S(1)} all-gather(f32[128,512]{1,0:T(8,128)S(1)} %pad_maximum_fusion.4), channel_id=1, replica_groups=mesh['dom'=32,'y'=8,'c'=2] {'c'}, dimensions={0}, use_global_device_ids=true | all-gather | bytes 786432 | tf_op jit(solution)/shard_map/all_gather | solution.py:31
  27.2 0.7 collective-permute-start.9
  28.0 2.2 %all_gather.22 = f32[256,512]{1,0:T(8,128)S(1)} all-gather(f32[128,512]{1,0:T(8,128)S(1)} %pad_maximum_fusion.1), channel_id=1, replica_groups=mesh['dom'=32,'y'=8,'c'=2] {'c'}, dimensions={0}, use_global_device_ids=true | all-gather | bytes 786432 | tf_op jit(solution)/shard_map/all_gather | solution.py:31
  30.2 2.2 %all_gather.23 = f32[256,512]{1,0:T(8,128)S(1)} all-gather(f32[128,512]{1,0:T(8,128)S(1)} %pad_maximum_fusion.2), channel_id=1, replica_groups=mesh['dom'=32,'y'=8,'c'=2] {'c'}, dimensions={0}, use_global_device_ids=true | all-gather | bytes 786432 | tf_op jit(solution)/shard_map/all_gather | solution.py:31
  33.1 0.7 collective-permute-start.4
  33.8 2.9 %bitcast_select_fusion.1 = (f32[256,512]{1,0:T(8,128)S(1)}, f32[256,512]{1,0:T(8,128)S(1)}, f32[256,512]{1,0:T(8,128)S(1)}, f32[256,512]{1,0:T(8,128)S(1)}, f32[...) fusion(f32[5,256,512]{2,1,0:T(8,128)} %collective-permute-done.10, ...), kind=kLoop, calls=%fused_computation.35 | loop fusion | flops 1048576 | bytes 8388609 | tf_op jit(solution)/shard_map/jit(_where)/select_n | solution.py:132
  38.6 0.7 collective-permute-start.11
  39.3 0.7 collective-permute-start.12
  40.7 0.6 fusion.66
  41.9 0.7 collective-permute-start.17
  42.6 0.7 collective-permute-start.18
  43.9 0.6 fusion.68
  45.1 0.7 collective-permute-start.19
  45.8 0.7 collective-permute-start.20
  47.8 0.7 collective-permute-start.24
  48.4 0.7 collective-permute-start.21
  49.7 0.7 collective-permute-start.25
  50.4 0.7 collective-permute-start.13
  51.2 0.7 collective-permute-start.27
  51.8 0.7 collective-permute-start.26
  52.5 0.7 collective-permute-start.22
  53.3 0.7 collective-permute-start.29
  54.0 0.7 collective-permute-start.28
  54.7 0.7 collective-permute-start.23
  55.5 0.7 collective-permute-start.14
  56.3 0.7 collective-permute-start.30
  57.0 0.7 collective-permute-start.15
  57.8 1.6 collective-permute-start.16
  59.4 0.7 collective-permute-start.31
  60.1 79.5 %collective-permute-done.16 = f32[128,512]{1,0:T(8,128)S(1)} collective-permute-done((f32[128,512]{1,0:T(8,128)S(1)}, f32[128,512]{1,0:T(8,128)S(1)}, u32[]{:S(2)}, u32[]{:S(2)}) %collective-permute-start.16) | collective-permute-done | bytes 262176 | tf_op jit(solution)/shard_map/ppermute | solution.py:23
  139.7 17.2 %all_gather.26 = f32[256,512]{1,0:T(8,128)S(1)} all-gather(f32[128,512]{1,0:T(8,128)S(1)} %add.69), channel_id=1, replica_groups=mesh['dom'=32,'y'=8,'c'=2] {'c'}, dimensions={0}, use_global_device_ids=true | all-gather | bytes 786432 | tf_op jit(solution)/shard_map/all_gather | solution.py:31
  157.0 1.3 collective-permute-start.32
  159.1 8.6 %collective-permute-done.32 = f32[192,512]{1,0:T(8,128)S(1)} collective-permute-done((f32[192,512]{1,0:T(8,128)S(1)}, f32[192,512]{1,0:T(8,128)S(1)}, u32[]{:S(2)}, u32[]{:S(2)}) %collective-permute-start.32) | collective-permute-done | bytes 393248 | tf_op jit(solution)/shard_map/ppermute | solution.py:23
  167.8 4.6 %all_gather.27 = f32[384,512]{1,0:T(8,128)S(1)} all-gather(f32[192,512]{1,0:T(8,128)S(1)} %add.83), channel_id=1, replica_groups=mesh['dom'=32,'y'=8,'c'=2] {'c'}, dimensions={0}, use_global_device_ids=true | all-gather | bytes 1179648 | tf_op jit(solution)/shard_map/all_gather | solution.py:31
  173.8 0.8 copy.6
  (92 shorter events, 10.5 us)
Async XLA Ops:
  1.0 13.8 %collective-permute-start.6 = (f32[64,512]{1,0:T(8,128)S(1)}, f32[64,512]{1,0:T(8,128)S(1)}, u32[]{:S(2)}, u32[]{:S(2)}) collective-permute-start(f32[64,512]{1,0:T(8,128)S(1)} %get-tuple-element.23), channel_id=1, source_target_pairs={{26,16},{27,17},{18,14},{19,15},{42,32},{43,33},{34,30},{35,31},{5... | collective-permute-start | bytes 393224 | tf_op jit(solution)/shard_map/ppermute | solution.py:23
  1.7 13.8 %collective-permute-start.5 = (f32[64,512]{1,0:T(8,128)S(1)}, f32[64,512]{1,0:T(8,128)S(1)}, u32[]{:S(2)}, u32[]{:S(2)}) collective-permute-start(f32[64,512]{1,0:T(8,128)S(1)} %get-tuple-element.23), channel_id=1, source_target_pairs={{24,16},{25,17},{16,14},{17,15},{40,32},{41,33},{32,30},{33,31},{5... | collective-permute-start | bytes 393224 | tf_op jit(solution)/shard_map/ppermute | solution.py:23
  2.3 16.0 %collective-permute-start.8 = (f32[64,512]{1,0:T(8,128)S(1)}, f32[64,512]{1,0:T(8,128)S(1)}, u32[]{:S(2)}, u32[]{:S(2)}) collective-permute-start(f32[64,512]{1,0:T(8,128)S(1)} %get-tuple-element.23), channel_id=1, source_target_pairs={{30,16},{31,17},{22,14},{23,15},{46,32},{47,33},{38,30},{39,31},{6... | collective-permute-start | bytes 393224 | tf_op jit(solution)/shard_map/ppermute | solution.py:23
  7.4 11.6 %collective-permute-start.7 = (f32[64,512]{1,0:T(8,128)S(1)}, f32[64,512]{1,0:T(8,128)S(1)}, u32[]{:S(2)}, u32[]{:S(2)}) collective-permute-start(f32[64,512]{1,0:T(8,128)S(1)} %get-tuple-element.23), channel_id=1, source_target_pairs={{28,16},{29,17},{20,14},{21,15},{44,32},{45,33},{36,30},{37,31},{6... | collective-permute-start | bytes 393224 | tf_op jit(solution)/shard_map/ppermute | solution.py:23
  8.1 19.1 %collective-permute-start.3 = (f32[64,512]{1,0:T(8,128)S(1)}, f32[64,512]{1,0:T(8,128)S(1)}, u32[]{:S(2)}, u32[]{:S(2)}) collective-permute-start(f32[64,512]{1,0:T(8,128)S(1)} %get-tuple-element.24), channel_id=1, source_target_pairs={{22,16},{23,17},{30,14},{31,15},{38,32},{39,33},{46,30},{47,31},{5... | collective-permute-start | bytes 393224 | tf_op jit(solution)/shard_map/ppermute | solution.py:23
  14.8 13.1 %collective-permute-start.2 = (f32[64,512]{1,0:T(8,128)S(1)}, f32[64,512]{1,0:T(8,128)S(1)}, u32[]{:S(2)}, u32[]{:S(2)}) collective-permute-start(f32[64,512]{1,0:T(8,128)S(1)} %get-tuple-element.24), channel_id=1, source_target_pairs={{20,16},{21,17},{28,14},{29,15},{36,32},{37,33},{44,30},{45,31},{5... | collective-permute-start | bytes 393224 | tf_op jit(solution)/shard_map/ppermute | solution.py:23
  15.5 12.4 %collective-permute-start.1 = (f32[64,512]{1,0:T(8,128)S(1)}, f32[64,512]{1,0:T(8,128)S(1)}, u32[]{:S(2)}, u32[]{:S(2)}) collective-permute-start(f32[64,512]{1,0:T(8,128)S(1)} %get-tuple-element.24), channel_id=1, source_target_pairs={{18,16},{19,17},{26,14},{27,15},{34,32},{35,33},{42,30},{43,31},{5... | collective-permute-start | bytes 393224 | tf_op jit(solution)/shard_map/ppermute | solution.py:23
  18.4 9.6 %collective-permute-start = (f32[64,512]{1,0:T(8,128)S(1)}, f32[64,512]{1,0:T(8,128)S(1)}, u32[]{:S(2)}, u32[]{:S(2)}) collective-permute-start(f32[64,512]{1,0:T(8,128)S(1)} %get-tuple-element.24), channel_id=1, source_target_pairs={{16,16},{17,17},{24,14},{25,15},{32,32},{33,33},{40,30},{41,31},{4... | collective-permute-start | bytes 393224 | tf_op jit(solution)/shard_map/ppermute | solution.py:23
  19.1 14.8 %collective-permute-start.10 = (f32[5,256,512]{2,1,0:T(8,128)}, f32[5,256,512]{2,1,0:T(8,128)}, u32[]{:S(2)}, u32[]{:S(2)}) collective-permute-start(f32[5,256,512]{2,1,0:T(8,128)} %param.4), channel_id=1, source_target_pairs={{0,1},{1,0},{2,3},{3,2},{4,5},{5,4},{6,7},{7,6},{8,9},{9,8},{10,11... | collective-permute-start | bytes 7864328 | tf_op jit(solution)/shard_map/ppermute | solution.py:27
  27.2 6.6 %collective-permute-start.9 = (f32[64,512]{1,0:T(8,128)S(1)}, f32[64,512]{1,0:T(8,128)S(1)}, u32[]{:S(2)}, u32[]{:S(2)}) collective-permute-start(f32[64,512]{1,0:T(8,128)S(1)} %fusion.43), channel_id=1, source_target_pairs={{16,0},{17,1},{14,30},{15,31},{48,32},{49,33},{46,62},{47,63},{80,... | collective-permute-start | bytes 393224 | tf_op jit(solution)/shard_map/ppermute | solution.py:23
  33.1 0.7 collective-permute-start.4
  38.6 1.4 collective-permute-start.11
  39.3 0.7 collective-permute-start.12
  41.9 1.4 collective-permute-start.17
  42.6 0.7 collective-permute-start.18
  45.1 1.4 collective-permute-start.19
  45.8 0.7 collective-permute-start.20
  47.8 1.4 collective-permute-start.24
  48.4 2.7 %collective-permute-start.21 = (f32[64,512]{1,0:T(8,128)S(1)}, f32[64,512]{1,0:T(8,128)S(1)}, u32[]{:S(2)}, u32[]{:S(2)}) collective-permute-start(f32[64,512]{1,0:T(8,128)S(1)} %add.71), channel_id=1, source_target_pairs={{0,64},{1,65},{126,62},{127,63},{128,192},{129,193},{254,190},{255... | collective-permute-start | bytes 393224 | tf_op jit(solution)/shard_map/ppermute | solution.py:23
  49.7 1.4 collective-permute-start.25
  50.4 2.8 %collective-permute-start.13 = (f32[64,512]{1,0:T(8,128)S(1)}, f32[64,512]{1,0:T(8,128)S(1)}, u32[]{:S(2)}, u32[]{:S(2)}) collective-permute-start(f32[64,512]{1,0:T(8,128)S(1)} %add.65), channel_id=1, source_target_pairs={{0,16},{1,17},{30,14},{31,15},{32,48},{33,49},{62,46},{63,47},{64,... | collective-permute-start | bytes 393224 | tf_op jit(solution)/shard_map/ppermute | solution.py:23
  51.2 2.1 %collective-permute-start.27 = (f32[64,512]{1,0:T(8,128)S(1)}, f32[64,512]{1,0:T(8,128)S(1)}, u32[]{:S(2)}, u32[]{:S(2)}) collective-permute-start(f32[64,512]{1,0:T(8,128)S(1)} %add.76), channel_id=1, source_target_pairs={{256,336},{257,337},{254,174},{255,175},{384,464},{385,465},{126,4... | collective-permute-start | bytes 393224 | tf_op jit(solution)/shard_map/ppermute | solution.py:23
  51.8 1.4 collective-permute-start.26
  52.5 2.1 %collective-permute-start.22 = (f32[128,512]{1,0:T(8,128)S(1)}, f32[128,512]{1,0:T(8,128)S(1)}, u32[]{:S(2)}, u32[]{:S(2)}) collective-permute-start(f32[128,512]{1,0:T(8,128)S(1)} %pad_maximum_fusion.6), channel_id=1, source_target_pairs={{0,32},{1,33},{62,30},{63,31},{64,96},{65,97},{126,94},{127,95},{1... | collective-permute-start | bytes 786440 | tf_op jit(solution)/shard_map/ppermute | solution.py:23
  53.3 2.8 %collective-permute-start.29 = (f32[64,512]{1,0:T(8,128)S(1)}, f32[64,512]{1,0:T(8,128)S(1)}, u32[]{:S(2)}, u32[]{:S(2)}) collective-permute-start(f32[64,512]{1,0:T(8,128)S(1)} %add_add_fusion.1), channel_id=1, source_target_pairs={{256,368},{257,369},{254,142},{255,143},{304,288},{305,289},{206,2... | collective-permute-start | bytes 393224 | tf_op jit(solution)/shard_map/ppermute | solution.py:23
  54.0 2.1 %collective-permute-start.28 = (f32[64,512]{1,0:T(8,128)S(1)}, f32[64,512]{1,0:T(8,128)S(1)}, u32[]{:S(2)}, u32[]{:S(2)}) collective-permute-start(f32[64,512]{1,0:T(8,128)S(1)} %add_add_fusion.1), channel_id=1, source_target_pairs={{256,272},{257,273},{254,238},{255,239},{304,320},{305,321},{206,1... | collective-permute-start | bytes 393224 | tf_op jit(solution)/shard_map/ppermute | solution.py:23
  54.7 1.5 collective-permute-start.23
  55.5 1.5 collective-permute-start.14
  56.3 3.1 %collective-permute-start.30 = (f32[192,512]{1,0:T(8,128)S(1)}, f32[192,512]{1,0:T(8,128)S(1)}, u32[]{:S(2)}, u32[]{:S(2)}) collective-permute-start(f32[192,512]{1,0:T(8,128)S(1)} %pad_maximum_fusion), channel_id=1, source_target_pairs={{0,14},{1,15},{14,0},{15,1},{16,30},{17,31},{30,16},{31,17},{32,46... | collective-permute-start | bytes 1179656 | tf_op jit(solution)/shard_map/ppermute | solution.py:23
  57.0 0.7 collective-permute-start.15
  57.8 100.5 %copy-start = (f32[5,256,512]{2,1,0:T(8,128)S(1)}, f32[5,256,512]{2,1,0:T(8,128)}, u32[]{:S(2)}) copy-start(f32[5,256,512]{2,1,0:T(8,128)} %param.4) | copy-start | bytes 7864324
  57.8 81.9 %collective-permute-start.16 = (f32[128,512]{1,0:T(8,128)S(1)}, f32[128,512]{1,0:T(8,128)S(1)}, u32[]{:S(2)}, u32[]{:S(2)}) collective-permute-start(f32[128,512]{1,0:T(8,128)S(1)} %add.68), channel_id=1, source_target_pairs={{0,2},{1,3},{4,6},{5,7},{14,12},{15,13},{10,8},{11,9},{16,18},{17,... | collective-permute-start | bytes 786440 | tf_op jit(solution)/shard_map/ppermute | solution.py:23
  59.4 97.5 %collective-permute-start.31 = (f32[192,512]{1,0:T(8,128)S(1)}, f32[192,512]{1,0:T(8,128)S(1)}, u32[]{:S(2)}, u32[]{:S(2)}) collective-permute-start(f32[192,512]{1,0:T(8,128)S(1)} %fusion.60), channel_id=1, source_target_pairs={{0,4},{1,5},{14,10},{15,11},{16,20},{17,21},{30,26},{31,27},{32,36... | collective-permute-start | bytes 1179656 | tf_op jit(solution)/shard_map/ppermute | solution.py:23
  157.0 10.8 %collective-permute-start.32 = (f32[192,512]{1,0:T(8,128)S(1)}, f32[192,512]{1,0:T(8,128)S(1)}, u32[]{:S(2)}, u32[]{:S(2)}) collective-permute-start(f32[192,512]{1,0:T(8,128)S(1)} %add.82), channel_id=1, source_target_pairs={{0,2},{1,3},{4,6},{5,7},{14,12},{15,13},{10,8},{11,9},{16,18},{17,... | collective-permute-start | bytes 1179656 | tf_op jit(solution)/shard_map/ppermute | solution.py:23

commit v3 on v2

--- a/solution.py
+++ b/solution.py
@@ -70,13 +70,6 @@
     return links
 
 
-def partner_links(parts, step):
-    links = []
-    for p in range(step, parts, step):
-        links += [(upper(p), lower(p)), (lower(p), upper(p))]
-    return links
-
-
 def corner_links(parts, bit):
     step = 1 << bit
     low = 2 * step - 1
@@ -92,9 +85,14 @@
 def top_links(parts, moves):
     p = parts // 2
     links = []
-    for a, b in moves:
-        links += [((p + a, 0), (p + b, 0)), ((p - 1 - a, LAST), (p - 1 - b, LAST))]
+    for (a, y), (b, w) in moves:
+        links += [((p + a, y), (p + b, w)), ((p - 1 - a, LAST - y), (p - 1 - b, LAST - w))]
     return links
+
+
+def line_links(parts, moves):
+    lines = [(n, y) for n in range(0, parts // 2, RING) for y in (0, LAST)]
+    return top_links(parts, [((n + a, y), (n + b, y)) for n, y in lines for a, b in moves])
 
 
 def chip_links(parts, pairs):
@@ -128,50 +126,51 @@
     own = lax.dynamic_slice_in_dim(both.T, mine, right_side.shape[1] // CORES, 0)
     here, there = spikes, swap_cores(spikes)
     tip_spikes = [
-        jnp.concatenate(
-            [jnp.where(first_core, here[k], there[k]), jnp.where(first_core, there[k], here[k])], axis=0
-        )
+        jnp.concatenate([jnp.where(first_core, here[k], there[k]), jnp.where(first_core, there[k], here[k])], axis=0)
         for k in range(top)
     ]
 
     held = []
     for level in range(levels):
-        near = dot_t(own, stay)
-        if level == top:
-            far = dot_t(own, go)
-            break
-        solved = permute(near, cross_links(parts, level))
-        far = dot_t(own, go)
-        solved = solved + permute(far, along_links(parts, level))
-        own = own - dot_t(solved, tip_spikes[level])
+        if level < top:
+            links = cross_links(parts, level), along_links(parts, level)
+        else:
+            p = parts // 2
+            links = (
+                [(upper(p), (p, LAST)), (lower(p), (p - 1, 0))],
+                [(upper(p), (p - 1, 0)), (lower(p), (p, LAST))],
+            )
+        solved = permute(dot_t(own, stay), links[0])
+        solved = solved + permute(dot_t(own, go), links[1])
         held.append(solved)
+        if level < top:
+            own = own - dot_t(solved, tip_spikes[level])
 
     def spread_chips(value):
-        for pairs in (ENDS, INNER, REST):
+        for pairs in (INNER, REST):
             value = value + permute(value, chip_links(parts, pairs))
         return value
 
+    def spread_ends(value):
+        return value + permute(value, chip_links(parts, ENDS))
+
     width = solved.shape[0]
     moved = held[1] + permute(held[1], corner_links(parts, 0))
-    low = spread_chips(jnp.concatenate([held[0], moved], axis=0))
+    low = spread_chips(spread_ends(jnp.concatenate([held[0], moved], axis=0)))
     third = held[3] + permute(held[3], corner_links(parts, 2))
     third = jnp.concatenate([held[2], third], axis=0)
     for bit in (1, 0):
         third = third + permute(third, corner_links(parts, bit))
 
-    p = parts // 2
-    at_root = (lax.axis_index("y") == 0) & (lax.axis_index("dom") == p)
-    at_root |= (lax.axis_index("y") == LAST) & (lax.axis_index("dom") == p - 1)
-    solved = jnp.where(at_root, near, 0.0) + permute(far, partner_links(parts, p))
-    last = solved + permute(solved, top_links(parts, [(0, RING)]))
-    lines = range(0, p, RING)
-    for k, (starts, ends) in enumerate(((((0, 3), (0, 5)), ()), (((0, 1), (3, 4), (5, 6)), ((0, 7), (3, 2))))):
-        if k == 0:
-            sets = [[starts[0]], [starts[1]]]
-        else:
-            sets = [starts, ends]
-        got = [permute(last, top_links(parts, [(n + a, n + b) for n in lines for a, b in moves])) for moves in sets]
-        last = last + got[0] + got[1]
+    third = spread_ends(third)
+
+    last = held[top]
+    root = (0, LAST)
+    got = [permute(last, top_links(parts, [(root, to)])) for to in ((RING, 0), (RING, LAST), (0, 0))]
+    last = last + got[0] + got[1] + got[2]
+    for ups, downs in ((((0, 3),), ((0, 5),)), (((0, 1), (3, 4), (5, 6)), ((0, 7), (3, 2)))):
+        up = permute(last, line_links(parts, ups))
+        last = last + up + permute(last, line_links(parts, downs))
     pair = spread_chips(jnp.concatenate([third, last], axis=0))
 
     def spread_update(out, level, full):

time: 175 us -> 159 us (0.909)
  the two profiles are of different devices: /device:TPU:159 before, /device:TPU:13 now
where the time goes in v3:
time: 159 us; the launch traced here: 158 us
  waiting for transfers between devices  65.2 us (41%)
  starting transfers between devices  44.5 us (28%)
  blocking collectives  29.9 us (19%)
  matrix products  10.7 us (7%)
  other arithmetic  4.68 us (3%)
  local copies, waits for them, and re-layouts  2.05 us (1%)
    ppermute x35, waiting for transfers between devices, permute(): return lax.ppermute(value, AXES, both_cores(links))  65.2 us
    ppermute x35, starting transfers between devices, permute(): return lax.ppermute(value, AXES, both_cores(links))  42.2 us
    all_gather x7, blocking collectives, cores_gather(): return lax.all_gather(value, 'c', axis=0, tiled=True)  29.9 us
    dot_general x14, matrix products, dot_t(): lax.dot_general(a, b, (((1,), (1,)), ((), ())), precision=MODE, preferred...  8.59 us
  transfers between devices with their start and end apart: 36, of which 2 were waited for; matrix products, arithmetic and copies ran while one was open for 5% of the time, Pallas kernels for 0%

profile of v3, /device:TPU:13, one launch (start us, length us, event | category | flops | bytes accessed | tf_op | source)
XLA Modules:
  0.0 158.0 jit_solution(8772498216813265723)
XLA Ops:
  0.0 1.0 slice_select_fusion
  1.0 13.4 %collective-permute-start.6 = (f32[64,512]{1,0:T(8,128)S(1)}, f32[64,512]{1,0:T(8,128)S(1)}, u32[]{:S(2)}, u32[]{:S(2)}) collective-permute-start(f32[64,512]{1,0:T(8,128)S(1)} %get-tuple-element.23), channel_id=1, source_target_pairs={{26,16},{27,17},{18,14},{19,15},{42,32},{43,33},{34,30},{35,31},{5... | collective-permute-start | bytes 393224 | tf_op jit(solution)/shard_map/ppermute | solution.py:23
  14.4 0.7 collective-permute-start.5
  15.1 0.7 collective-permute-start.8
  15.8 0.7 collective-permute-start.7
  16.5 0.7 collective-permute-start.3
  17.1 1.0 copy.5
  18.2 2.6 %all_gather.21 = f32[512,128]{0,1:T(8,128)S(1)} all-gather(f32[256,128]{0,1:T(8,128)S(1)} %copy.5), channel_id=1, replica_groups=mesh['dom'=32,'y'=8,'c'=2] {'c'}, dimensions={0}, use_global_device_ids=true | all-gather | bytes 393216 | tf_op jit(solution)/shard_map/all_gather | solution.py:31
  20.7 0.7 collective-permute-start.2
  21.4 5.3 %collective-permute-start.1 = (f32[64,512]{1,0:T(8,128)S(1)}, f32[64,512]{1,0:T(8,128)S(1)}, u32[]{:S(2)}, u32[]{:S(2)}) collective-permute-start(f32[64,512]{1,0:T(8,128)S(1)} %get-tuple-element.24), channel_id=1, source_target_pairs={{18,16},{19,17},{26,14},{27,15},{34,32},{35,33},{42,30},{43,31},{5... | collective-permute-start | bytes 393224 | tf_op jit(solution)/shard_map/ppermute | solution.py:23
  26.8 2.5 %all_gather.24 = f32[256,512]{1,0:T(8,128)S(1)} all-gather(f32[128,512]{1,0:T(8,128)S(1)} %pad_maximum_fusion.3), channel_id=1, replica_groups=mesh['dom'=32,'y'=8,'c'=2] {'c'}, dimensions={0}, use_global_device_ids=true | all-gather | bytes 786432 | tf_op jit(solution)/shard_map/all_gather | solution.py:31
  29.9 2.3 %collective-permute-start.10 = (f32[5,256,512]{2,1,0:T(8,128)}, f32[5,256,512]{2,1,0:T(8,128)}, u32[]{:S(2)}, u32[]{:S(2)}) collective-permute-start(f32[5,256,512]{2,1,0:T(8,128)} %param.4), channel_id=1, source_target_pairs={{0,1},{1,0},{2,3},{3,2},{4,5},{5,4},{6,7},{7,6},{8,9},{9,8},{10,11... | collective-permute-start | bytes 7864328 | tf_op jit(solution)/shard_map/ppermute | solution.py:27
  32.2 5.1 %all_gather.25 = f32[256,512]{1,0:T(8,128)S(1)} all-gather(f32[128,512]{1,0:T(8,128)S(1)} %pad_maximum_fusion.4), channel_id=1, replica_groups=mesh['dom'=32,'y'=8,'c'=2] {'c'}, dimensions={0}, use_global_device_ids=true | all-gather | bytes 786432 | tf_op jit(solution)/shard_map/all_gather | solution.py:31
  38.1 0.7 collective-permute-start.9
  38.8 2.2 %all_gather.22 = f32[256,512]{1,0:T(8,128)S(1)} all-gather(f32[128,512]{1,0:T(8,128)S(1)} %pad_maximum_fusion.1), channel_id=1, replica_groups=mesh['dom'=32,'y'=8,'c'=2] {'c'}, dimensions={0}, use_global_device_ids=true | all-gather | bytes 786432 | tf_op jit(solution)/shard_map/all_gather | solution.py:31
  41.0 2.2 %all_gather.23 = f32[256,512]{1,0:T(8,128)S(1)} all-gather(f32[128,512]{1,0:T(8,128)S(1)} %pad_maximum_fusion.2), channel_id=1, replica_groups=mesh['dom'=32,'y'=8,'c'=2] {'c'}, dimensions={0}, use_global_device_ids=true | all-gather | bytes 786432 | tf_op jit(solution)/shard_map/all_gather | solution.py:31
  43.9 0.7 collective-permute-start.4
  44.7 2.9 %bitcast_select_fusion.1 = (f32[256,512]{1,0:T(8,128)S(1)}, f32[256,512]{1,0:T(8,128)S(1)}, f32[256,512]{1,0:T(8,128)S(1)}, f32[256,512]{1,0:T(8,128)S(1)}, f32[...) fusion(f32[5,256,512]{2,1,0:T(8,128)} %collective-permute-done.10, ...), kind=kLoop, calls=%fused_computation.33 | loop fusion | flops 1048576 | bytes 8388609 | tf_op jit(solution)/shard_map/jit(_where)/select_n | solution.py:129
  49.5 0.7 collective-permute-start.11
  50.1 0.7 collective-permute-start.12
  52.7 0.7 collective-permute-start.17
  53.4 0.7 collective-permute-start.18
  54.1 0.7 collective-permute-start.13
  56.6 0.7 collective-permute-start.19
  57.3 0.7 collective-permute-start.20
  58.0 0.7 collective-permute-start.14
  60.6 0.7 collective-permute-start.25
  61.3 0.7 collective-permute-start.26
  62.0 0.7 collective-permute-start.21
  62.7 0.7 collective-permute-start.29
  63.4 0.7 collective-permute-start.28
  64.0 0.7 collective-permute-start.27
  64.8 0.7 collective-permute-start.22
  65.5 0.7 collective-permute-start.15
  66.3 0.7 collective-permute-start.31
  67.0 0.7 collective-permute-start.30
  67.7 0.7 collective-permute-start.23
  68.4 0.7 collective-permute-start.33
  69.1 0.7 collective-permute-start.32
  69.9 0.7 collective-permute-start.24
  70.6 1.3 collective-permute-start.16
  72.1 0.8 collective-permute-start.34
  72.9 55.5 %collective-permute-done.16 = f32[128,512]{1,0:T(8,128)S(1)} collective-permute-done((f32[128,512]{1,0:T(8,128)S(1)}, f32[128,512]{1,0:T(8,128)S(1)}, u32[]{:S(2)}, u32[]{:S(2)}) %collective-permute-start.16) | collective-permute-done | bytes 262176 | tf_op jit(solution)/shard_map/ppermute | solution.py:23
  128.4 11.9 %all_gather.26 = f32[256,512]{1,0:T(8,128)S(1)} all-gather(f32[128,512]{1,0:T(8,128)S(1)} %add.75), channel_id=1, replica_groups=mesh['dom'=32,'y'=8,'c'=2] {'c'}, dimensions={0}, use_global_device_ids=true | all-gather | bytes 786432 | tf_op jit(solution)/shard_map/all_gather | solution.py:31
  140.4 1.3 collective-permute-start.35
  142.5 9.7 %collective-permute-done.35 = f32[192,512]{1,0:T(8,128)S(1)} collective-permute-done((f32[192,512]{1,0:T(8,128)S(1)}, f32[192,512]{1,0:T(8,128)S(1)}, u32[]{:S(2)}, u32[]{:S(2)}) %collective-permute-start.35) | collective-permute-done | bytes 393248 | tf_op jit(solution)/shard_map/ppermute | solution.py:23
  152.3 3.6 %all_gather.27 = f32[384,512]{1,0:T(8,128)S(1)} all-gather(f32[192,512]{1,0:T(8,128)S(1)} %add.91), channel_id=1, replica_groups=mesh['dom'=32,'y'=8,'c'=2] {'c'}, dimensions={0}, use_global_device_ids=true | all-gather | bytes 1179648 | tf_op jit(solution)/shard_map/all_gather | solution.py:31
  157.2 0.8 copy.6
  (99 shorter events, 12.4 us)
Async XLA Ops:
  1.0 19.7 %collective-permute-start.6 = (f32[64,512]{1,0:T(8,128)S(1)}, f32[64,512]{1,0:T(8,128)S(1)}, u32[]{:S(2)}, u32[]{:S(2)}) collective-permute-start(f32[64,512]{1,0:T(8,128)S(1)} %get-tuple-element.23), channel_id=1, source_target_pairs={{26,16},{27,17},{18,14},{19,15},{42,32},{43,33},{34,30},{35,31},{5... | collective-permute-start | bytes 393224 | tf_op jit(solution)/shard_map/ppermute | solution.py:23
  14.4 7.0 %collective-permute-start.5 = (f32[64,512]{1,0:T(8,128)S(1)}, f32[64,512]{1,0:T(8,128)S(1)}, u32[]{:S(2)}, u32[]{:S(2)}) collective-permute-start(f32[64,512]{1,0:T(8,128)S(1)} %get-tuple-element.23), channel_id=1, source_target_pairs={{24,16},{25,17},{16,14},{17,15},{40,32},{41,33},{32,30},{33,31},{5... | collective-permute-start | bytes 393224 | tf_op jit(solution)/shard_map/ppermute | solution.py:23
  15.1 14.1 %collective-permute-start.8 = (f32[64,512]{1,0:T(8,128)S(1)}, f32[64,512]{1,0:T(8,128)S(1)}, u32[]{:S(2)}, u32[]{:S(2)}) collective-permute-start(f32[64,512]{1,0:T(8,128)S(1)} %get-tuple-element.23), channel_id=1, source_target_pairs={{30,16},{31,17},{22,14},{23,15},{46,32},{47,33},{38,30},{39,31},{6... | collective-permute-start | bytes 393224 | tf_op jit(solution)/shard_map/ppermute | solution.py:23
  15.8 14.1 %collective-permute-start.7 = (f32[64,512]{1,0:T(8,128)S(1)}, f32[64,512]{1,0:T(8,128)S(1)}, u32[]{:S(2)}, u32[]{:S(2)}) collective-permute-start(f32[64,512]{1,0:T(8,128)S(1)} %get-tuple-element.23), channel_id=1, source_target_pairs={{28,16},{29,17},{20,14},{21,15},{44,32},{45,33},{36,30},{37,31},{6... | collective-permute-start | bytes 393224 | tf_op jit(solution)/shard_map/ppermute | solution.py:23
  16.5 21.6 %collective-permute-start.3 = (f32[64,512]{1,0:T(8,128)S(1)}, f32[64,512]{1,0:T(8,128)S(1)}, u32[]{:S(2)}, u32[]{:S(2)}) collective-permute-start(f32[64,512]{1,0:T(8,128)S(1)} %get-tuple-element.24), channel_id=1, source_target_pairs={{22,16},{23,17},{30,14},{31,15},{38,32},{39,33},{46,30},{47,31},{5... | collective-permute-start | bytes 393224 | tf_op jit(solution)/shard_map/ppermute | solution.py:23
  20.7 18.0 %collective-permute-start.2 = (f32[64,512]{1,0:T(8,128)S(1)}, f32[64,512]{1,0:T(8,128)S(1)}, u32[]{:S(2)}, u32[]{:S(2)}) collective-permute-start(f32[64,512]{1,0:T(8,128)S(1)} %get-tuple-element.24), channel_id=1, source_target_pairs={{20,16},{21,17},{28,14},{29,15},{36,32},{37,33},{44,30},{45,31},{5... | collective-permute-start | bytes 393224 | tf_op jit(solution)/shard_map/ppermute | solution.py:23
  21.4 17.4 %collective-permute-start.1 = (f32[64,512]{1,0:T(8,128)S(1)}, f32[64,512]{1,0:T(8,128)S(1)}, u32[]{:S(2)}, u32[]{:S(2)}) collective-permute-start(f32[64,512]{1,0:T(8,128)S(1)} %get-tuple-element.24), channel_id=1, source_target_pairs={{18,16},{19,17},{26,14},{27,15},{34,32},{35,33},{42,30},{43,31},{5... | collective-permute-start | bytes 393224 | tf_op jit(solution)/shard_map/ppermute | solution.py:23
  29.2 9.6 %collective-permute-start = (f32[64,512]{1,0:T(8,128)S(1)}, f32[64,512]{1,0:T(8,128)S(1)}, u32[]{:S(2)}, u32[]{:S(2)}) collective-permute-start(f32[64,512]{1,0:T(8,128)S(1)} %get-tuple-element.24), channel_id=1, source_target_pairs={{16,16},{17,17},{24,14},{25,15},{32,32},{33,33},{40,30},{41,31},{4... | collective-permute-start | bytes 393224 | tf_op jit(solution)/shard_map/ppermute | solution.py:23
  29.9 14.8 %collective-permute-start.10 = (f32[5,256,512]{2,1,0:T(8,128)}, f32[5,256,512]{2,1,0:T(8,128)}, u32[]{:S(2)}, u32[]{:S(2)}) collective-permute-start(f32[5,256,512]{2,1,0:T(8,128)} %param.4), channel_id=1, source_target_pairs={{0,1},{1,0},{2,3},{3,2},{4,5},{5,4},{6,7},{7,6},{8,9},{9,8},{10,11... | collective-permute-start | bytes 7864328 | tf_op jit(solution)/shard_map/ppermute | solution.py:27
  38.1 6.6 %collective-permute-start.9 = (f32[64,512]{1,0:T(8,128)S(1)}, f32[64,512]{1,0:T(8,128)S(1)}, u32[]{:S(2)}, u32[]{:S(2)}) collective-permute-start(f32[64,512]{1,0:T(8,128)S(1)} %fusion.42), channel_id=1, source_target_pairs={{16,0},{17,1},{14,30},{15,31},{48,32},{49,33},{46,62},{47,63},{80,... | collective-permute-start | bytes 393224 | tf_op jit(solution)/shard_map/ppermute | solution.py:23
  43.9 0.7 collective-permute-start.4
  49.5 1.4 collective-permute-start.11
  50.1 0.7 collective-permute-start.12
  52.7 2.0 %collective-permute-start.17 = (f32[64,512]{1,0:T(8,128)S(1)}, f32[64,512]{1,0:T(8,128)S(1)}, u32[]{:S(2)}, u32[]{:S(2)}) collective-permute-start(f32[64,512]{1,0:T(8,128)S(1)} %fusion.64), channel_id=1, source_target_pairs={{64,126},{65,127},{62,0},{63,1},{192,254},{193,255},{190,128},{191... | collective-permute-start | bytes 393224 | tf_op jit(solution)/shard_map/ppermute | solution.py:23
  53.4 1.4 collective-permute-start.18
  54.1 3.9 %collective-permute-start.13 = (f32[64,512]{1,0:T(8,128)S(1)}, f32[64,512]{1,0:T(8,128)S(1)}, u32[]{:S(2)}, u32[]{:S(2)}) collective-permute-start(f32[64,512]{1,0:T(8,128)S(1)} %add.71), channel_id=1, source_target_pairs={{0,16},{1,17},{30,14},{31,15},{32,48},{33,49},{62,46},{63,47},{64,... | collective-permute-start | bytes 393224 | tf_op jit(solution)/shard_map/ppermute | solution.py:23
  56.6 2.1 %collective-permute-start.19 = (f32[64,512]{1,0:T(8,128)S(1)}, f32[64,512]{1,0:T(8,128)S(1)}, u32[]{:S(2)}, u32[]{:S(2)}) collective-permute-start(f32[64,512]{1,0:T(8,128)S(1)} %fusion.66), channel_id=1, source_target_pairs={{128,254},{129,255},{126,0},{127,1},{384,510},{385,511},{382,256},... | collective-permute-start | bytes 393224 | tf_op jit(solution)/shard_map/ppermute | solution.py:23
  57.3 1.4 collective-permute-start.20
  58.0 7.4 %collective-permute-start.14 = (f32[128,512]{1,0:T(8,128)S(1)}, f32[128,512]{1,0:T(8,128)S(1)}, u32[]{:S(2)}, u32[]{:S(2)}) collective-permute-start(f32[128,512]{1,0:T(8,128)S(1)} %pad_maximum_fusion.5), channel_id=1, source_target_pairs={{0,14},{1,15},{14,0},{15,1},{16,30},{17,31},{30,16},{31,17},{32,46... | collective-permute-start | bytes 786440 | tf_op jit(solution)/shard_map/ppermute | solution.py:23
  60.6 2.0 %collective-permute-start.25 = (f32[64,512]{1,0:T(8,128)S(1)}, f32[64,512]{1,0:T(8,128)S(1)}, u32[]{:S(2)}, u32[]{:S(2)}) collective-permute-start(f32[64,512]{1,0:T(8,128)S(1)} %fusion.68), channel_id=1, source_target_pairs={{256,270},{257,271},{254,240},{255,241}} | collective-permute-start | bytes 393224 | tf_op jit(solution)/shard_map/ppermute | solution.py:23
  61.3 1.4 collective-permute-start.26
  62.0 2.8 %collective-permute-start.21 = (f32[64,512]{1,0:T(8,128)S(1)}, f32[64,512]{1,0:T(8,128)S(1)}, u32[]{:S(2)}, u32[]{:S(2)}) collective-permute-start(f32[64,512]{1,0:T(8,128)S(1)} %add.77), channel_id=1, source_target_pairs={{0,64},{1,65},{126,62},{127,63},{128,192},{129,193},{254,190},{255... | collective-permute-start | bytes 393224 | tf_op jit(solution)/shard_map/ppermute | solution.py:23
  62.7 3.5 %collective-permute-start.29 = (f32[64,512]{1,0:T(8,128)S(1)}, f32[64,512]{1,0:T(8,128)S(1)}, u32[]{:S(2)}, u32[]{:S(2)}) collective-permute-start(f32[64,512]{1,0:T(8,128)S(1)} %add.82), channel_id=1, source_target_pairs={{270,256},{271,257},{240,254},{241,255}} | collective-permute-start | bytes 393224 | tf_op jit(solution)/shard_map/ppermute | solution.py:23
  63.4 2.9 %collective-permute-start.28 = (f32[64,512]{1,0:T(8,128)S(1)}, f32[64,512]{1,0:T(8,128)S(1)}, u32[]{:S(2)}, u32[]{:S(2)}) collective-permute-start(f32[64,512]{1,0:T(8,128)S(1)} %add.82), channel_id=1, source_target_pairs={{270,398},{271,399},{240,112},{241,113}} | collective-permute-start | bytes 393224 | tf_op jit(solution)/shard_map/ppermute | solution.py:23
  64.0 2.2 %collective-permute-start.27 = (f32[64,512]{1,0:T(8,128)S(1)}, f32[64,512]{1,0:T(8,128)S(1)}, u32[]{:S(2)}, u32[]{:S(2)}) collective-permute-start(f32[64,512]{1,0:T(8,128)S(1)} %add.82), channel_id=1, source_target_pairs={{270,384},{271,385},{240,126},{241,127}} | collective-permute-start | bytes 393224 | tf_op jit(solution)/shard_map/ppermute | solution.py:23
  64.8 2.9 %collective-permute-start.22 = (f32[128,512]{1,0:T(8,128)S(1)}, f32[128,512]{1,0:T(8,128)S(1)}, u32[]{:S(2)}, u32[]{:S(2)}) collective-permute-start(f32[128,512]{1,0:T(8,128)S(1)} %pad_maximum_fusion.6), channel_id=1, source_target_pairs={{0,32},{1,33},{62,30},{63,31},{64,96},{65,97},{126,94},{127,95},{1... | collective-permute-start | bytes 786440 | tf_op jit(solution)/shard_map/ppermute | solution.py:23
  65.5 5.0 %collective-permute-start.15 = (f32[128,512]{1,0:T(8,128)S(1)}, f32[128,512]{1,0:T(8,128)S(1)}, u32[]{:S(2)}, u32[]{:S(2)}) collective-permute-start(f32[128,512]{1,0:T(8,128)S(1)} %fusion.58), channel_id=1, source_target_pairs={{0,4},{1,5},{14,10},{15,11},{16,20},{17,21},{30,26},{31,27},{32,36... | collective-permute-start | bytes 786440 | tf_op jit(solution)/shard_map/ppermute | solution.py:23
  66.3 2.1 %collective-permute-start.31 = (f32[64,512]{1,0:T(8,128)S(1)}, f32[64,512]{1,0:T(8,128)S(1)}, u32[]{:S(2)}, u32[]{:S(2)}) collective-permute-start(f32[64,512]{1,0:T(8,128)S(1)} %add_add_fusion.2), channel_id=1, source_target_pairs={{256,336},{257,337},{254,174},{255,175},{270,350},{271,351},{240,1... | collective-permute-start | bytes 393224 | tf_op jit(solution)/shard_map/ppermute | solution.py:23
  67.0 1.4 collective-permute-start.30
  67.7 2.1 %collective-permute-start.23 = (f32[128,512]{1,0:T(8,128)S(1)}, f32[128,512]{1,0:T(8,128)S(1)}, u32[]{:S(2)}, u32[]{:S(2)}) collective-permute-start(f32[128,512]{1,0:T(8,128)S(1)} %fusion.57), channel_id=1, source_target_pairs={{0,16},{1,17},{30,14},{31,15},{32,48},{33,49},{62,46},{63,47},{64,... | collective-permute-start | bytes 786440 | tf_op jit(solution)/shard_map/ppermute | solution.py:23
  68.4 3.5 %collective-permute-start.33 = (f32[64,512]{1,0:T(8,128)S(1)}, f32[64,512]{1,0:T(8,128)S(1)}, u32[]{:S(2)}, u32[]{:S(2)}) collective-permute-start(f32[64,512]{1,0:T(8,128)S(1)} %add_add_fusion.1), channel_id=1, source_target_pairs={{256,368},{257,369},{254,142},{255,143},{304,288},{305,289},{206,2... | collective-permute-start | bytes 393224 | tf_op jit(solution)/shard_map/ppermute | solution.py:23
  69.1 2.8 %collective-permute-start.32 = (f32[64,512]{1,0:T(8,128)S(1)}, f32[64,512]{1,0:T(8,128)S(1)}, u32[]{:S(2)}, u32[]{:S(2)}) collective-permute-start(f32[64,512]{1,0:T(8,128)S(1)} %add_add_fusion.1), channel_id=1, source_target_pairs={{256,272},{257,273},{254,238},{255,239},{304,320},{305,321},{206,1... | collective-permute-start | bytes 393224 | tf_op jit(solution)/shard_map/ppermute | solution.py:23
  69.9 2.1 %collective-permute-start.24 = (f32[128,512]{1,0:T(8,128)S(1)}, f32[128,512]{1,0:T(8,128)S(1)}, u32[]{:S(2)}, u32[]{:S(2)}) collective-permute-start(f32[128,512]{1,0:T(8,128)S(1)} %add.80), channel_id=1, source_target_pairs={{0,14},{1,15},{14,0},{15,1},{16,30},{17,31},{30,16},{31,17},{32,46... | collective-permute-start | bytes 786440 | tf_op jit(solution)/shard_map/ppermute | solution.py:23
  70.6 57.8 %collective-permute-start.16 = (f32[128,512]{1,0:T(8,128)S(1)}, f32[128,512]{1,0:T(8,128)S(1)}, u32[]{:S(2)}, u32[]{:S(2)}) collective-permute-start(f32[128,512]{1,0:T(8,128)S(1)} %add.74), channel_id=1, source_target_pairs={{0,2},{1,3},{4,6},{5,7},{14,12},{15,13},{10,8},{11,9},{16,18},{17,... | collective-permute-start | bytes 786440 | tf_op jit(solution)/shard_map/ppermute | solution.py:23
  72.0 69.7 %copy-start = (f32[5,256,512]{2,1,0:T(8,128)S(1)}, f32[5,256,512]{2,1,0:T(8,128)}, u32[]{:S(2)}) copy-start(f32[5,256,512]{2,1,0:T(8,128)} %param.4) | copy-start | bytes 7864324
  72.1 68.3 %collective-permute-start.34 = (f32[192,512]{1,0:T(8,128)S(1)}, f32[192,512]{1,0:T(8,128)S(1)}, u32[]{:S(2)}, u32[]{:S(2)}) collective-permute-start(f32[192,512]{1,0:T(8,128)S(1)} %pad_maximum_fusion), channel_id=1, source_target_pairs={{0,4},{1,5},{14,10},{15,11},{16,20},{17,21},{30,26},{31,27},{32,36... | collective-permute-start | bytes 1179656 | tf_op jit(solution)/shard_map/ppermute | solution.py:23
  140.4 11.8 %collective-permute-start.35 = (f32[192,512]{1,0:T(8,128)S(1)}, f32[192,512]{1,0:T(8,128)S(1)}, u32[]{:S(2)}, u32[]{:S(2)}) collective-permute-start(f32[192,512]{1,0:T(8,128)S(1)} %fusion.59), channel_id=1, source_target_pairs={{0,2},{1,3},{4,6},{5,7},{14,12},{15,13},{10,8},{11,9},{16,18},{17,... | collective-permute-start | bytes 1179656 | tf_op jit(solution)/shard_map/ppermute | solution.py:23

commit v4 on v3

--- a/solution.py
+++ b/solution.py
@@ -31,8 +31,20 @@
     return lax.all_gather(value, "c", axis=0, tiled=True)
 
 
-def dot_t(a, b):
-    return lax.dot_general(a, b, (((1,), (1,)), ((), ())), precision=MODE, preferred_element_type=jnp.float32)
+def split(value):
+    high = lax.reduce_precision(value, 8, 7)
+    return high.astype(jnp.bfloat16), (value - high).astype(jnp.bfloat16)
+
+
+def split_matrix(value):
+    high, low = split(value)
+    return jnp.concatenate([high, high, low], axis=1)
+
+
+def dot_split(value, matrix):
+    high, low = split(value)
+    wide = jnp.concatenate([high, low, high], axis=1)
+    return lax.dot_general(wide, matrix, (((1,), (1,)), ((), ())), preferred_element_type=jnp.float32)
 
 
 def boundaries(parts, level):
@@ -47,10 +59,19 @@
     return (p - 1, LAST)
 
 
+RELAYED = (3, 4, 5, 6)
+ARRIVAL = (3, 4, 5, 6, 0, 1, 2, 7)
+
+
+def relay_links(parts):
+    return [((p, m), (p - 1, m)) for p in range(1, parts) for m in RELAYED]
+
+
 def inverse_links(parts, j):
+    m = (j + CHIPS // 2) % CHIPS
     links = []
     for p in range(1, parts):
-        links += [((p, j), upper(p)), ((p, (j + CHIPS // 2) % CHIPS), lower(p))]
+        links += [((p, j), upper(p)), ((p - 1 if m in RELAYED else p, m), lower(p))]
     return links
 
 
@@ -70,15 +91,30 @@
     return links
 
 
-def corner_links(parts, bit):
+def halving_links(parts, level, bit):
     step = 1 << bit
     low = 2 * step - 1
     links = []
     for q in range(parts):
-        if q & low == low:
-            links.append(((q, LAST), (q - step, LAST)))
-        if q & low == 0:
-            links.append(((q, 0), (q + step, 0)))
+        for y in (0, LAST):
+            if q >> level & 1 and q & low == low:
+                links.append(((q, y), (q - step, y)))
+            if not q >> level & 1 and q & low == 0:
+                links.append(((q, y), (q + step, y)))
+    return links
+
+
+def neighbour_links(parts):
+    return [((q, y), (q ^ 1, y)) for q in range(parts) for y in (0, LAST)]
+
+
+def ring_links(moves, roots):
+    links = []
+    for n, from_last in enumerate(roots):
+        for a, b in moves:
+            if from_last:
+                a, b = RING - 1 - a, RING - 1 - b
+            links += [((RING * n + a, y), (RING * n + b, y)) for y in (0, LAST)]
     return links
 
 
@@ -88,11 +124,6 @@
     for (a, y), (b, w) in moves:
         links += [((p + a, y), (p + b, w)), ((p - 1 - a, LAST - y), (p - 1 - b, LAST - w))]
     return links
-
-
-def line_links(parts, moves):
-    lines = [(n, y) for n in range(0, parts // 2, RING) for y in (0, LAST)]
-    return top_links(parts, [((n + a, y), (n + b, y)) for n, y in lines for a, b in moves])
 
 
 def chip_links(parts, pairs):
@@ -113,20 +144,27 @@
 
     inverse = inverses[0]
     below, above = inverse[:, :cols], inverse[:, cols:]
-    for_upper = lax.axis_index("y") < CHIPS // 2
-    sent = jnp.where(for_upper, above, below), jnp.where(for_upper, below, above)
-    pieces = [permute(sent[j // (CHIPS // 2)], inverse_links(parts, j)) for j in range(CHIPS)]
-    blocks = []
-    for j in range(0, CHIPS, 2):
-        gathered = cores_gather(jnp.concatenate(pieces[j : j + 2], axis=0))
-        blocks += [jnp.split(gathered, 4, axis=0)[i] for i in (0, 2, 1, 3)]
-    stay, go = jnp.concatenate(blocks[:CHIPS], axis=0), jnp.concatenate(blocks[CHIPS:], axis=0)
+    chip = lax.axis_index("y")
+    direct = (chip >= RELAYED[0]) & (chip <= RELAYED[-1])
+    relayed = permute(below, relay_links(parts))
+    sent = jnp.where(direct, above, below), jnp.where(direct, relayed, above)
+    pieces = [permute(sent[n // (CHIPS // 2)], inverse_links(parts, j)) for n, j in enumerate(ARRIVAL)]
+    blocks = [None] * (2 * CHIPS)
+    for n in range(0, CHIPS, 2):
+        gathered = cores_gather(jnp.concatenate(pieces[n : n + 2], axis=0))
+        for i, block in enumerate(jnp.split(gathered, 4, axis=0)):
+            blocks[2 * ARRIVAL[n + i % 2] + i // 2] = block
+    stay, go = (split_matrix(jnp.concatenate(half, axis=0)) for half in (blocks[:CHIPS], blocks[CHIPS:]))
 
     both = cores_gather(right_side)
     own = lax.dynamic_slice_in_dim(both.T, mine, right_side.shape[1] // CORES, 0)
     here, there = spikes, swap_cores(spikes)
     tip_spikes = [
-        jnp.concatenate([jnp.where(first_core, here[k], there[k]), jnp.where(first_core, there[k], here[k])], axis=0)
+        split_matrix(
+            jnp.concatenate(
+                [jnp.where(first_core, here[k], there[k]), jnp.where(first_core, there[k], here[k])], axis=0
+            )
+        )
         for k in range(top)
     ]
 
@@ -140,11 +178,13 @@
                 [(upper(p), (p, LAST)), (lower(p), (p - 1, 0))],
                 [(upper(p), (p - 1, 0)), (lower(p), (p, LAST))],
             )
-        solved = permute(dot_t(own, stay), links[0])
-        solved = solved + permute(dot_t(own, go), links[1])
-        held.append(solved)
+        solved = permute(dot_split(own, stay), links[0])
+        leaving = dot_split(own, go)
+        solved = solved + permute(leaving, links[1])
+        held.append(lax.optimization_barrier(solved))
         if level < top:
-            own = own - dot_t(solved, tip_spikes[level])
+            change = dot_split(solved, tip_spikes[level])
+            own = own - change
 
     def spread_chips(value):
         for pairs in (INNER, REST):
@@ -154,24 +194,31 @@
     def spread_ends(value):
         return value + permute(value, chip_links(parts, ENDS))
 
+    def spread_rings(value, roots):
+        rounds = ((((0, 3),), ((0, 5),)), (((0, 1), (3, 4), (5, 6)), ((0, 7), (3, 2))))
+        for ups, downs in rounds:
+            up = permute(value, ring_links(ups, roots))
+            value = value + up + permute(value, ring_links(downs, roots))
+        return value
+
     width = solved.shape[0]
-    moved = held[1] + permute(held[1], corner_links(parts, 0))
-    low = spread_chips(spread_ends(jnp.concatenate([held[0], moved], axis=0)))
-    third = held[3] + permute(held[3], corner_links(parts, 2))
-    third = jnp.concatenate([held[2], third], axis=0)
-    for bit in (1, 0):
-        third = third + permute(third, corner_links(parts, bit))
-
-    third = spread_ends(third)
+    low = spread_ends(jnp.concatenate(held[:2], axis=0))
+    first = low[width:]
+    first = first + permute(first, neighbour_links(parts))
+    low = spread_chips(jnp.concatenate([low[:width], first], axis=0))
+    second = spread_ends(held[2])
+    second = second + permute(second, halving_links(parts, 2, 1))
+    second = second + permute(second, neighbour_links(parts))
+    third = spread_ends(held[3])
+    for bit in (2, 1):
+        third = third + permute(third, halving_links(parts, 3, bit))
+    third = third + permute(third, neighbour_links(parts))
+    pair = jnp.concatenate([second, third], axis=0)
 
     last = held[top]
-    root = (0, LAST)
-    got = [permute(last, top_links(parts, [(root, to)])) for to in ((RING, 0), (RING, LAST), (0, 0))]
-    last = last + got[0] + got[1] + got[2]
-    for ups, downs in ((((0, 3),), ((0, 5),)), (((0, 1), (3, 4), (5, 6)), ((0, 7), (3, 2)))):
-        up = permute(last, line_links(parts, ups))
-        last = last + up + permute(last, line_links(parts, downs))
-    pair = spread_chips(jnp.concatenate([third, last], axis=0))
+    got = [permute(last, top_links(parts, [((0, LAST), to)])) for to in ((RING, 0), (RING, LAST), (0, 0))]
+    last = spread_rings(last + got[0] + got[1] + got[2], (True, True, False, False))
+    pair = spread_chips(jnp.concatenate([pair, last], axis=0))
 
     def spread_update(out, level, full):
         return out - lax.dot_general(

time: 159 us -> 174 us (1.094)
  waiting for transfers between devices: 65.2 us -> 80.8 us
  blocking collectives: 29.9 us -> 23.5 us
  local copies, waits for them, and re-layouts: 2.05 us -> 4.39 us
    ppermute x35 -> x39, waiting for transfers between devices: 65.2 us -> 80.8 us  [permute(): return lax.ppermute(value, AXES, both_cores(links))]
    all_gather x7, blocking collectives: 29.9 us -> 23.5 us  [cores_gather(): return lax.all_gather(value, 'c', axis=0, tiled=True)]
    convert_element_type x0 -> x15, other arithmetic: none -> 2.07 us  [split(): return (high.astype(jnp.bfloat16), (value - high).astype(jnp.bfloat16))]
    ppermute x35 -> x39, starting transfers between devices: 42.2 us -> 43.3 us  [permute(): return lax.ppermute(value, AXES, both_cores(links))]
  transfers between devices with their start and end apart: 36 -> 40, of which waited for: 2 -> 2; matrix products, arithmetic and copies ran while one was open for 5% -> 6% of each run, Pallas kernels for 0% -> 0%
where the time goes in v4:
time: 174 us; the launch traced here: 173 us
  waiting for transfers between devices  80.8 us (46%)
  starting transfers between devices  45.9 us (26%)
  blocking collectives  23.5 us (14%)
  matrix products  11.7 us (7%)
  other arithmetic  5.93 us (3%)
  local copies, waits for them, and re-layouts  4.39 us (3%)
    ppermute x39, waiting for transfers between devices, permute(): return lax.ppermute(value, AXES, both_cores(links))  80.8 us
    ppermute x39, starting transfers between devices, permute(): return lax.ppermute(value, AXES, both_cores(links))  43.3 us
    all_gather x7, blocking collectives, cores_gather(): return lax.all_gather(value, 'c', axis=0, tiled=True)  23.5 us
    dot_general x14, matrix products, dot_split(): lax.dot_general(wide, matrix, (((1,), (1,)), ((), ())), preferred_element...  9.64 us
  transfers between devices with their start and end apart: 40, of which 2 were waited for; matrix products, arithmetic and copies ran while one was open for 6% of the time, Pallas kernels for 0%

profile of v4, /device:TPU:13, one launch (start us, length us, event | category | flops | bytes accessed | tf_op | source)
XLA Modules:
  0.0 173.3 jit_solution(13924727857269268670)
XLA Ops:
  0.0 0.9 slice.104
  0.9 0.7 collective-permute-start
  1.6 2.6 %collective-permute-start.11 = (f32[5,256,512]{2,1,0:T(8,128)}, f32[5,256,512]{2,1,0:T(8,128)}, u32[]{:S(2)}, u32[]{:S(2)}) collective-permute-start(f32[5,256,512]{2,1,0:T(8,128)} %param.4), channel_id=1, source_target_pairs={{0,1},{1,0},{2,3},{3,2},{4,5},{5,4},{6,7},{7,6},{8,9},{9,8},{10,11... | collective-permute-start | bytes 7864328 | tf_op jit(solution)/shard_map/ppermute | solution.py:27
  4.2 1.0 copy.5
  5.2 1.0 slice_select_fusion
  6.2 2.1 %collective-permute-start.2 = (f32[64,512]{1,0:T(8,128)S(1)}, f32[64,512]{1,0:T(8,128)S(1)}, u32[]{:S(2)}, u32[]{:S(2)}) collective-permute-start(f32[64,512]{1,0:T(8,128)S(1)} %get-tuple-element.50), channel_id=1, source_target_pairs={{18,16},{19,17},{10,14},{11,15},{34,32},{35,33},{26,30},{27,31},{5... | collective-permute-start | bytes 393224 | tf_op jit(solution)/shard_map/ppermute | solution.py:23
  8.3 0.7 collective-permute-start.1
  9.0 2.0 %all_gather.21 = f32[512,128]{0,1:T(8,128)S(1)} all-gather(f32[256,128]{0,1:T(8,128)S(1)} %copy.5), channel_id=1, replica_groups=mesh['dom'=32,'y'=8,'c'=2] {'c'}, dimensions={0}, use_global_device_ids=true | all-gather | bytes 393216 | tf_op jit(solution)/shard_map/all_gather | solution.py:31
  11.0 0.7 collective-permute-start.9
  11.7 13.9 %collective-permute-start.8 = (f32[64,512]{1,0:T(8,128)S(1)}, f32[64,512]{1,0:T(8,128)S(1)}, u32[]{:S(2)}, u32[]{:S(2)}) collective-permute-start(f32[64,512]{1,0:T(8,128)S(1)} %get-tuple-element.49), channel_id=1, source_target_pairs={{26,16},{27,17},{18,14},{19,15},{42,32},{43,33},{34,30},{35,31},{5... | collective-permute-start | bytes 393224 | tf_op jit(solution)/shard_map/ppermute | solution.py:23
  25.6 0.7 collective-permute-start.6
  26.3 0.7 collective-permute-start.5
  27.0 2.2 %all_gather.22 = f32[256,512]{1,0:T(8,128)S(1)} all-gather(f32[128,512]{1,0:T(8,128)S(1)} %pad_maximum_fusion.7), channel_id=1, replica_groups=mesh['dom'=32,'y'=8,'c'=2] {'c'}, dimensions={0}, use_global_device_ids=true | all-gather | bytes 786432 | tf_op jit(solution)/shard_map/all_gather | solution.py:31
  29.9 0.7 collective-permute-start.3
  30.6 2.2 %all_gather.24 = f32[256,512]{1,0:T(8,128)S(1)} all-gather(f32[128,512]{1,0:T(8,128)S(1)} %pad_maximum_fusion.9), channel_id=1, replica_groups=mesh['dom'=32,'y'=8,'c'=2] {'c'}, dimensions={0}, use_global_device_ids=true | all-gather | bytes 786432 | tf_op jit(solution)/shard_map/all_gather | solution.py:31
  32.8 2.2 %all_gather.25 = f32[256,512]{1,0:T(8,128)S(1)} all-gather(f32[128,512]{1,0:T(8,128)S(1)} %pad_maximum_fusion.10), channel_id=1, replica_groups=mesh['dom'=32,'y'=8,'c'=2] {'c'}, dimensions={0}, use_global_device_ids=true | all-gather | bytes 786432 | tf_op jit(solution)/shard_map/all_gather | solution.py:31
  35.2 2.2 %all_gather.23 = f32[256,512]{1,0:T(8,128)S(1)} all-gather(f32[128,512]{1,0:T(8,128)S(1)} %pad_maximum_fusion.8), channel_id=1, replica_groups=mesh['dom'=32,'y'=8,'c'=2] {'c'}, dimensions={0}, use_global_device_ids=true | all-gather | bytes 786432 | tf_op jit(solution)/shard_map/all_gather | solution.py:31
  37.6 1.2 fusion.109
  38.9 1.3 collective-permute-start.10
  40.4 0.8 copy-done.3
  41.2 1.2 fusion.110
  42.5 1.3 collective-permute-start.7
  43.8 1.0 fusion.93
  44.8 2.2 %bitcast_select_fusion.1 = (f32[256,512]{1,0:T(8,128)S(1)}, f32[256,512]{1,0:T(8,128)S(1)}, f32[256,512]{1,0:T(8,128)S(1)}, f32[256,512]{1,0:T(8,128)S(1)}, f32[...) fusion(f32[5,256,512]{2,1,0:T(8,128)} %collective-permute-done.11, ...), kind=kLoop, calls=%fused_computation.69 | loop fusion | flops 1048576 | bytes 8388609 | tf_op jit(solution)/shard_map/jit(_where)/select_n | solution.py:165
  49.6 0.7 collective-permute-start.12
  50.3 0.7 collective-permute-start.13
  53.0 0.7 collective-permute-start.18
  53.7 0.7 collective-permute-start.19
  56.4 0.7 collective-permute-start.23
  57.1 0.7 collective-permute-start.24
  58.0 0.7 collective-permute-start.14
  58.7 0.7 collective-permute-start.20
  61.9 0.7 collective-permute-start.30
  62.6 0.7 collective-permute-start.15
  63.3 0.7 collective-permute-start.25
  64.0 0.7 collective-permute-start.21
  64.7 0.7 collective-permute-start.33
  65.4 0.7 collective-permute-start.32
  69.0 0.7 collective-permute-start.34
  69.7 0.7 collective-permute-start.16
  73.3 1.3 collective-permute-start.17
  74.8 0.7 collective-permute-start.38
  75.4 70.6 %collective-permute-done.17 = f32[128,512]{1,0:T(8,128)S(1)} collective-permute-done((f32[128,512]{1,0:T(8,128)S(1)}, f32[128,512]{1,0:T(8,128)S(1)}, u32[]{:S(2)}, u32[]{:S(2)}) %collective-permute-start.17) | collective-permute-done | bytes 262176 | tf_op jit(solution)/shard_map/ppermute | solution.py:23
  146.1 9.5 %all_gather.26 = f32[256,512]{1,0:T(8,128)S(1)} all-gather(f32[128,512]{1,0:T(8,128)S(1)} %add.84), channel_id=1, replica_groups=mesh['dom'=32,'y'=8,'c'=2] {'c'}, dimensions={0}, use_global_device_ids=true | all-gather | bytes 786432 | tf_op jit(solution)/shard_map/all_gather | solution.py:31
  155.8 1.3 collective-permute-start.39
  157.9 10.1 %collective-permute-done.39 = f32[192,512]{1,0:T(8,128)S(1)} collective-permute-done((f32[192,512]{1,0:T(8,128)S(1)}, f32[192,512]{1,0:T(8,128)S(1)}, u32[]{:S(2)}, u32[]{:S(2)}) %collective-permute-start.39) | collective-permute-done | bytes 393248 | tf_op jit(solution)/shard_map/ppermute | solution.py:23
  168.0 3.2 %all_gather.27 = f32[384,512]{1,0:T(8,128)S(1)} all-gather(f32[192,512]{1,0:T(8,128)S(1)} %add.103), channel_id=1, replica_groups=mesh['dom'=32,'y'=8,'c'=2] {'c'}, dimensions={0}, use_global_device_ids=true | all-gather | bytes 1179648 | tf_op jit(solution)/shard_map/all_gather | solution.py:31
  172.6 0.8 copy.6
  (133 shorter events, 18.6 us)
Async XLA Ops:
  0.9 4.3 %collective-permute-start = (f32[64,512]{1,0:T(8,128)S(1)}, f32[64,512]{1,0:T(8,128)S(1)}, u32[]{:S(2)}, u32[]{:S(2)}) collective-permute-start(f32[64,512]{1,0:T(8,128)S(1)} %slice.104), channel_id=1, source_target_pairs={{22,6},{23,7},{24,8},{25,9},{26,10},{27,11},{28,12},{29,13},{38,22... | collective-permute-start | bytes 393224 | tf_op jit(solution)/shard_map/ppermute | solution.py:23
  1.6 43.2 %collective-permute-start.11 = (f32[5,256,512]{2,1,0:T(8,128)}, f32[5,256,512]{2,1,0:T(8,128)}, u32[]{:S(2)}, u32[]{:S(2)}) collective-permute-start(f32[5,256,512]{2,1,0:T(8,128)} %param.4), channel_id=1, source_target_pairs={{0,1},{1,0},{2,3},{3,2},{4,5},{5,4},{6,7},{7,6},{8,9},{9,8},{10,11... | collective-permute-start | bytes 7864328 | tf_op jit(solution)/shard_map/ppermute | solution.py:27
  6.2 19.4 %collective-permute-start.2 = (f32[64,512]{1,0:T(8,128)S(1)}, f32[64,512]{1,0:T(8,128)S(1)}, u32[]{:S(2)}, u32[]{:S(2)}) collective-permute-start(f32[64,512]{1,0:T(8,128)S(1)} %get-tuple-element.50), channel_id=1, source_target_pairs={{18,16},{19,17},{10,14},{11,15},{34,32},{35,33},{26,30},{27,31},{5... | collective-permute-start | bytes 393224 | tf_op jit(solution)/shard_map/ppermute | solution.py:23
  8.3 18.0 %collective-permute-start.1 = (f32[64,512]{1,0:T(8,128)S(1)}, f32[64,512]{1,0:T(8,128)S(1)}, u32[]{:S(2)}, u32[]{:S(2)}) collective-permute-start(f32[64,512]{1,0:T(8,128)S(1)} %get-tuple-element.50), channel_id=1, source_target_pairs={{16,16},{17,17},{8,14},{9,15},{32,32},{33,33},{24,30},{25,31},{48,... | collective-permute-start | bytes 393224 | tf_op jit(solution)/shard_map/ppermute | solution.py:23
  11.0 21.8 %collective-permute-start.9 = (f32[64,512]{1,0:T(8,128)S(1)}, f32[64,512]{1,0:T(8,128)S(1)}, u32[]{:S(2)}, u32[]{:S(2)}) collective-permute-start(f32[64,512]{1,0:T(8,128)S(1)} %get-tuple-element.49), channel_id=1, source_target_pairs={{28,16},{29,17},{20,14},{21,15},{44,32},{45,33},{36,30},{37,31},{6... | collective-permute-start | bytes 393224 | tf_op jit(solution)/shard_map/ppermute | solution.py:23
  11.7 21.1 %collective-permute-start.8 = (f32[64,512]{1,0:T(8,128)S(1)}, f32[64,512]{1,0:T(8,128)S(1)}, u32[]{:S(2)}, u32[]{:S(2)}) collective-permute-start(f32[64,512]{1,0:T(8,128)S(1)} %get-tuple-element.49), channel_id=1, source_target_pairs={{26,16},{27,17},{18,14},{19,15},{42,32},{43,33},{34,30},{35,31},{5... | collective-permute-start | bytes 393224 | tf_op jit(solution)/shard_map/ppermute | solution.py:23
  25.6 3.6 %collective-permute-start.6 = (f32[64,512]{1,0:T(8,128)S(1)}, f32[64,512]{1,0:T(8,128)S(1)}, u32[]{:S(2)}, u32[]{:S(2)}) collective-permute-start(f32[64,512]{1,0:T(8,128)S(1)} %get-tuple-element.49), channel_id=1, source_target_pairs={{24,16},{25,17},{16,14},{17,15},{40,32},{41,33},{32,30},{33,31},{5... | collective-permute-start | bytes 393224 | tf_op jit(solution)/shard_map/ppermute | solution.py:23
  26.3 3.6 %collective-permute-start.5 = (f32[64,512]{1,0:T(8,128)S(1)}, f32[64,512]{1,0:T(8,128)S(1)}, u32[]{:S(2)}, u32[]{:S(2)}) collective-permute-start(f32[64,512]{1,0:T(8,128)S(1)} %get-tuple-element.49), channel_id=1, source_target_pairs={{22,16},{23,17},{30,14},{31,15},{38,32},{39,33},{46,30},{47,31},{5... | collective-permute-start | bytes 393224 | tf_op jit(solution)/shard_map/ppermute | solution.py:23
  29.2 5.9 %collective-permute-start.4 = (f32[64,512]{1,0:T(8,128)S(1)}, f32[64,512]{1,0:T(8,128)S(1)}, u32[]{:S(2)}, u32[]{:S(2)}) collective-permute-start(f32[64,512]{1,0:T(8,128)S(1)} %get-tuple-element.50), channel_id=1, source_target_pairs={{30,16},{31,17},{6,14},{7,15},{46,32},{47,33},{22,30},{23,31},{62,... | collective-permute-start | bytes 393224 | tf_op jit(solution)/shard_map/ppermute | solution.py:23
  29.9 5.3 %collective-permute-start.3 = (f32[64,512]{1,0:T(8,128)S(1)}, f32[64,512]{1,0:T(8,128)S(1)}, u32[]{:S(2)}, u32[]{:S(2)}) collective-permute-start(f32[64,512]{1,0:T(8,128)S(1)} %get-tuple-element.50), channel_id=1, source_target_pairs={{20,16},{21,17},{12,14},{13,15},{36,32},{37,33},{28,30},{29,31},{5... | collective-permute-start | bytes 393224 | tf_op jit(solution)/shard_map/ppermute | solution.py:23
  37.6 2.8 %copy-start.1 = (bf16[512,512]{1,0:T(8,128)(2,1)}, bf16[512,512]{1,0:T(8,128)(2,1)S(1)}, u32[]{:S(2)}) copy-start(bf16[512,512]{1,0:T(8,128)(2,1)S(1)} %get-tuple-element.28) | copy-start | bytes 1572868
  38.9 4.9 %collective-permute-start.10 = (f32[64,512]{1,0:T(8,128)}, f32[64,512]{1,0:T(8,128)}, u32[]{:S(2)}, u32[]{:S(2)}) collective-permute-start(f32[64,512]{1,0:T(8,128)} %fusion.109), channel_id=1, source_target_pairs={{16,0},{17,1},{14,30},{15,31},{48,32},{49,33},{46,62},{47,63},{80,... | collective-permute-start | bytes 393224 | tf_op jit(solution)/shard_map/ppermute | solution.py:23
  40.4 0.8 copy-start.3
  40.4 2.1 %copy-start.5 = (bf16[512,512]{1,0:T(8,128)(2,1)}, bf16[512,512]{1,0:T(8,128)(2,1)S(1)}, u32[]{:S(2)}) copy-start(bf16[512,512]{1,0:T(8,128)(2,1)S(1)} %get-tuple-element.30) | copy-start | bytes 1572868
  40.4 4.4 %copy-start = (f32[5,256,512]{2,1,0:T(8,128)S(1)}, f32[5,256,512]{2,1,0:T(8,128)}, u32[]{:S(2)}) copy-start(f32[5,256,512]{2,1,0:T(8,128)} %param.4) | copy-start | bytes 7864324
  42.5 1.3 collective-permute-start.7
  47.2 1.0 copy-start.2
  47.8 1.1 copy-start.4
  47.8 1.2 copy-start.6
  49.6 1.5 collective-permute-start.12
  50.3 0.9 collective-permute-start.13
  53.0 1.5 collective-permute-start.18
  53.7 0.9 collective-permute-start.19
  56.4 2.9 %collective-permute-start.23 = (f32[64,512]{1,0:T(8,128)S(1)}, f32[64,512]{1,0:T(8,128)S(1)}, u32[]{:S(2)}, u32[]{:S(2)}) collective-permute-start(f32[64,512]{1,0:T(8,128)S(1)} %fusion.104), channel_id=1, source_target_pairs={{128,254},{129,255},{126,0},{127,1},{384,510},{385,511},{382,256},... | collective-permute-start | bytes 393224 | tf_op jit(solution)/shard_map/ppermute | solution.py:23
  57.1 2.2 %collective-permute-start.24 = (f32[64,512]{1,0:T(8,128)S(1)}, f32[64,512]{1,0:T(8,128)S(1)}, u32[]{:S(2)}, u32[]{:S(2)}) collective-permute-start(f32[64,512]{1,0:T(8,128)S(1)} %fusion.103), channel_id=1, source_target_pairs={{128,0},{129,1},{126,254},{127,255},{384,256},{385,257},{382,510},... | collective-permute-start | bytes 393224 | tf_op jit(solution)/shard_map/ppermute | solution.py:23
  58.0 4.6 %collective-permute-start.14 = (f32[128,512]{1,0:T(8,128)S(1)}, f32[128,512]{1,0:T(8,128)S(1)}, u32[]{:S(2)}, u32[]{:S(2)}) collective-permute-start(f32[128,512]{1,0:T(8,128)S(1)} %pad_maximum_fusion.11), channel_id=1, source_target_pairs={{0,14},{1,15},{14,0},{15,1},{16,30},{17,31},{30,16},{31,17},{32,46... | collective-permute-start | bytes 786440 | tf_op jit(solution)/shard_map/ppermute | solution.py:23
  58.7 5.3 %collective-permute-start.20 = (f32[64,512]{1,0:T(8,128)S(1)}, f32[64,512]{1,0:T(8,128)S(1)}, u32[]{:S(2)}, u32[]{:S(2)}) collective-permute-start(f32[64,512]{1,0:T(8,128)S(1)} %get-tuple-element.8), channel_id=1, source_target_pairs={{0,14},{1,15},{14,0},{15,1},{16,30},{17,31},{30,16},{31,17},{32,46... | collective-permute-start | bytes 393224 | tf_op jit(solution)/shard_map/ppermute | solution.py:23
  60.6 4.1 %collective-permute-start.29 = (f32[64,512]{1,0:T(8,128)S(1)}, f32[64,512]{1,0:T(8,128)S(1)}, u32[]{:S(2)}, u32[]{:S(2)}) collective-permute-start(f32[64,512]{1,0:T(8,128)S(1)} %fusion.102), channel_id=1, source_target_pairs={{256,270},{257,271},{254,240},{255,241}} | collective-permute-start | bytes 393224 | tf_op jit(solution)/shard_map/ppermute | solution.py:23
  61.9 2.8 %collective-permute-start.30 = (f32[64,512]{1,0:T(8,128)S(1)}, f32[64,512]{1,0:T(8,128)S(1)}, u32[]{:S(2)}, u32[]{:S(2)}) collective-permute-start(f32[64,512]{1,0:T(8,128)S(1)} %fusion.101), channel_id=1, source_target_pairs={{256,240},{257,241},{254,270},{255,271}} | collective-permute-start | bytes 393224 | tf_op jit(solution)/shard_map/ppermute | solution.py:23
  62.6 3.5 %collective-permute-start.15 = (f32[64,512]{1,0:T(8,128)S(1)}, f32[64,512]{1,0:T(8,128)S(1)}, u32[]{:S(2)}, u32[]{:S(2)}) collective-permute-start(f32[64,512]{1,0:T(8,128)S(1)} %slice.108), channel_id=1, source_target_pairs={{0,16},{1,17},{14,30},{15,31},{16,0},{17,1},{30,14},{31,15},{32,48... | collective-permute-start | bytes 393224 | tf_op jit(solution)/shard_map/ppermute | solution.py:23
  63.3 3.5 %collective-permute-start.25 = (f32[64,512]{1,0:T(8,128)S(1)}, f32[64,512]{1,0:T(8,128)S(1)}, u32[]{:S(2)}, u32[]{:S(2)}) collective-permute-start(f32[64,512]{1,0:T(8,128)S(1)} %get-tuple-element.6), channel_id=1, source_target_pairs={{0,14},{1,15},{14,0},{15,1},{16,30},{17,31},{30,16},{31,17},{32,46... | collective-permute-start | bytes 393224 | tf_op jit(solution)/shard_map/ppermute | solution.py:23
  64.0 3.5 %collective-permute-start.21 = (f32[64,512]{1,0:T(8,128)S(1)}, f32[64,512]{1,0:T(8,128)S(1)}, u32[]{:S(2)}, u32[]{:S(2)}) collective-permute-start(f32[64,512]{1,0:T(8,128)S(1)} %add.86), channel_id=1, source_target_pairs={{0,32},{1,33},{14,46},{15,47},{112,80},{113,81},{126,94},{127,95},... | collective-permute-start | bytes 393224 | tf_op jit(solution)/shard_map/ppermute | solution.py:23
  64.7 3.5 %collective-permute-start.33 = (f32[64,512]{1,0:T(8,128)S(1)}, f32[64,512]{1,0:T(8,128)S(1)}, u32[]{:S(2)}, u32[]{:S(2)}) collective-permute-start(f32[64,512]{1,0:T(8,128)S(1)} %add.94), channel_id=1, source_target_pairs={{270,256},{271,257},{240,254},{241,255}} | collective-permute-start | bytes 393224 | tf_op jit(solution)/shard_map/ppermute | solution.py:23
  65.4 2.8 %collective-permute-start.32 = (f32[64,512]{1,0:T(8,128)S(1)}, f32[64,512]{1,0:T(8,128)S(1)}, u32[]{:S(2)}, u32[]{:S(2)}) collective-permute-start(f32[64,512]{1,0:T(8,128)S(1)} %add.94), channel_id=1, source_target_pairs={{270,398},{271,399},{240,112},{241,113}} | collective-permute-start | bytes 393224 | tf_op jit(solution)/shard_map/ppermute | solution.py:23
  66.1 2.2 %collective-permute-start.31 = (f32[64,512]{1,0:T(8,128)S(1)}, f32[64,512]{1,0:T(8,128)S(1)}, u32[]{:S(2)}, u32[]{:S(2)}) collective-permute-start(f32[64,512]{1,0:T(8,128)S(1)} %add.94), channel_id=1, source_target_pairs={{270,384},{271,385},{240,126},{241,127}} | collective-permute-start | bytes 393224 | tf_op jit(solution)/shard_map/ppermute | solution.py:23
  66.8 3.5 %collective-permute-start.26 = (f32[64,512]{1,0:T(8,128)S(1)}, f32[64,512]{1,0:T(8,128)S(1)}, u32[]{:S(2)}, u32[]{:S(2)}) collective-permute-start(f32[64,512]{1,0:T(8,128)S(1)} %add.90), channel_id=1, source_target_pairs={{0,64},{1,65},{14,78},{15,79},{240,176},{241,177},{254,190},{255,1... | collective-permute-start | bytes 393224 | tf_op jit(solution)/shard_map/ppermute | solution.py:23
  67.6 3.5 %collective-permute-start.22 = (f32[64,512]{1,0:T(8,128)S(1)}, f32[64,512]{1,0:T(8,128)S(1)}, u32[]{:S(2)}, u32[]{:S(2)}) collective-permute-start(f32[64,512]{1,0:T(8,128)S(1)} %add.87), channel_id=1, source_target_pairs={{0,16},{1,17},{14,30},{15,31},{16,0},{17,1},{30,14},{31,15},{32,48... | collective-permute-start | bytes 393224 | tf_op jit(solution)/shard_map/ppermute | solution.py:23
  68.3 2.8 %collective-permute-start.35 = (f32[64,512]{1,0:T(8,128)S(1)}, f32[64,512]{1,0:T(8,128)S(1)}, u32[]{:S(2)}, u32[]{:S(2)}) collective-permute-start(f32[64,512]{1,0:T(8,128)S(1)} %add_add_fusion.2), channel_id=1, source_target_pairs={{112,32},{113,33},{126,46},{127,47},{240,160},{241,161},{254,174},... | collective-permute-start | bytes 393224 | tf_op jit(solution)/shard_map/ppermute | solution.py:23
  69.0 2.2 %collective-permute-start.34 = (f32[64,512]{1,0:T(8,128)S(1)}, f32[64,512]{1,0:T(8,128)S(1)}, u32[]{:S(2)}, u32[]{:S(2)}) collective-permute-start(f32[64,512]{1,0:T(8,128)S(1)} %add_add_fusion.2), channel_id=1, source_target_pairs={{112,64},{113,65},{126,78},{127,79},{240,192},{241,193},{254,206},... | collective-permute-start | bytes 393224 | tf_op jit(solution)/shard_map/ppermute | solution.py:23
  69.7 3.6 %collective-permute-start.16 = (f32[128,512]{1,0:T(8,128)S(1)}, f32[128,512]{1,0:T(8,128)S(1)}, u32[]{:S(2)}, u32[]{:S(2)}) collective-permute-start(f32[128,512]{1,0:T(8,128)S(1)} %pad_maximum_fusion.12), channel_id=1, source_target_pairs={{0,4},{1,5},{14,10},{15,11},{16,20},{17,21},{30,26},{31,27},{32,36... | collective-permute-start | bytes 786440 | tf_op jit(solution)/shard_map/ppermute | solution.py:23
  70.4 2.1 %collective-permute-start.27 = (f32[64,512]{1,0:T(8,128)S(1)}, f32[64,512]{1,0:T(8,128)S(1)}, u32[]{:S(2)}, u32[]{:S(2)}) collective-permute-start(f32[64,512]{1,0:T(8,128)S(1)} %add.91), channel_id=1, source_target_pairs={{0,32},{1,33},{14,46},{15,47},{64,96},{65,97},{78,110},{79,111},{1... | collective-permute-start | bytes 393224 | tf_op jit(solution)/shard_map/ppermute | solution.py:23
  71.2 3.5 %collective-permute-start.37 = (f32[64,512]{1,0:T(8,128)S(1)}, f32[64,512]{1,0:T(8,128)S(1)}, u32[]{:S(2)}, u32[]{:S(2)}) collective-permute-start(f32[64,512]{1,0:T(8,128)S(1)} %add_add_fusion.1), channel_id=1, source_target_pairs={{112,0},{113,1},{126,14},{127,15},{64,80},{65,81},{78,94},{79,95},... | collective-permute-start | bytes 393224 | tf_op jit(solution)/shard_map/ppermute | solution.py:23
  71.9 2.8 %collective-permute-start.36 = (f32[64,512]{1,0:T(8,128)S(1)}, f32[64,512]{1,0:T(8,128)S(1)}, u32[]{:S(2)}, u32[]{:S(2)}) collective-permute-start(f32[64,512]{1,0:T(8,128)S(1)} %add_add_fusion.1), channel_id=1, source_target_pairs={{112,96},{113,97},{126,110},{127,111},{64,48},{65,49},{78,62},{79,... | collective-permute-start | bytes 393224 | tf_op jit(solution)/shard_map/ppermute | solution.py:23
  72.6 2.0 %collective-permute-start.28 = (f32[64,512]{1,0:T(8,128)S(1)}, f32[64,512]{1,0:T(8,128)S(1)}, u32[]{:S(2)}, u32[]{:S(2)}) collective-permute-start(f32[64,512]{1,0:T(8,128)S(1)} %add.92), channel_id=1, source_target_pairs={{0,16},{1,17},{14,30},{15,31},{16,0},{17,1},{30,14},{31,15},{32,48... | collective-permute-start | bytes 393224 | tf_op jit(solution)/shard_map/ppermute | solution.py:23
  73.3 72.8 %collective-permute-start.17 = (f32[128,512]{1,0:T(8,128)S(1)}, f32[128,512]{1,0:T(8,128)S(1)}, u32[]{:S(2)}, u32[]{:S(2)}) collective-permute-start(f32[128,512]{1,0:T(8,128)S(1)} %fusion.130), channel_id=1, source_target_pairs={{0,2},{1,3},{4,6},{5,7},{14,12},{15,13},{10,8},{11,9},{16,18},{17,... | collective-permute-start | bytes 786440 | tf_op jit(solution)/shard_map/ppermute | solution.py:23
  74.8 80.9 %collective-permute-start.38 = (f32[192,512]{1,0:T(8,128)S(1)}, f32[192,512]{1,0:T(8,128)S(1)}, u32[]{:S(2)}, u32[]{:S(2)}) collective-permute-start(f32[192,512]{1,0:T(8,128)S(1)} %pad_maximum_fusion.6), channel_id=1, source_target_pairs={{0,4},{1,5},{14,10},{15,11},{16,20},{17,21},{30,26},{31,27},{32,36... | collective-permute-start | bytes 1179656 | tf_op jit(solution)/shard_map/ppermute | solution.py:23
  155.8 12.2 %collective-permute-start.39 = (f32[192,512]{1,0:T(8,128)S(1)}, f32[192,512]{1,0:T(8,128)S(1)}, u32[]{:S(2)}, u32[]{:S(2)}) collective-permute-start(f32[192,512]{1,0:T(8,128)S(1)} %fusion.132), channel_id=1, source_target_pairs={{0,2},{1,3},{4,6},{5,7},{14,12},{15,13},{10,8},{11,9},{16,18},{17,... | collective-permute-start | bytes 1179656 | tf_op jit(solution)/shard_map/ppermute | solution.py:23

commit v5 on v4

--- a/solution.py
+++ b/solution.py
@@ -188,7 +188,8 @@
 
     def spread_chips(value):
         for pairs in (INNER, REST):
-            value = value + permute(value, chip_links(parts, pairs))
+            got = permute(value, chip_links(parts, pairs))
+            value = value + got
         return value
 
     def spread_ends(value):
@@ -198,27 +199,26 @@
         rounds = ((((0, 3),), ((0, 5),)), (((0, 1), (3, 4), (5, 6)), ((0, 7), (3, 2))))
         for ups, downs in rounds:
             up = permute(value, ring_links(ups, roots))
-            value = value + up + permute(value, ring_links(downs, roots))
+            down = permute(value, ring_links(downs, roots))
+            value = value + up + down
         return value
 
     width = solved.shape[0]
     low = spread_ends(jnp.concatenate(held[:2], axis=0))
     first = low[width:]
     first = first + permute(first, neighbour_links(parts))
-    low = spread_chips(jnp.concatenate([low[:width], first], axis=0))
     second = spread_ends(held[2])
     second = second + permute(second, halving_links(parts, 2, 1))
     second = second + permute(second, neighbour_links(parts))
+    low = spread_chips(jnp.concatenate([low[:width], first, second], axis=0))
     third = spread_ends(held[3])
     for bit in (2, 1):
         third = third + permute(third, halving_links(parts, 3, bit))
     third = third + permute(third, neighbour_links(parts))
-    pair = jnp.concatenate([second, third], axis=0)
-
     last = held[top]
     got = [permute(last, top_links(parts, [((0, LAST), to)])) for to in ((RING, 0), (RING, LAST), (0, 0))]
     last = spread_rings(last + got[0] + got[1] + got[2], (True, True, False, False))
-    pair = spread_chips(jnp.concatenate([pair, last], axis=0))
+    pair = spread_chips(jnp.concatenate([third, last], axis=0))
 
     def spread_update(out, level, full):
         return out - lax.dot_general(
@@ -226,7 +226,7 @@
         )
 
     out = right_side
-    for value, first in ((low, 0), (pair, 2)):
+    for value, first in ((low, 0), (pair, 3)):
         count = value.shape[0] // width
         ends = cores_gather(value)
         for k in range(count):

time: 174 us -> 233 us (1.34)
  the two profiles are of different devices: /device:TPU:13 before, /device:TPU:1 now
where the time goes in v5:
time: 233 us; the launch traced here: 232 us
  starting transfers between devices  121 us (52%)
  waiting for transfers between devices  62.7 us (27%)
  blocking collectives  25.8 us (11%)
  matrix products  11.7 us (5%)
  other arithmetic  5.92 us (3%)
  local copies, waits for them, and re-layouts  4.39 us (2%)
    ppermute x39, starting transfers between devices, permute(): return lax.ppermute(value, AXES, both_cores(links))  103 us
    ppermute x39, waiting for transfers between devices, permute(): return lax.ppermute(value, AXES, both_cores(links))  62.7 us
    all_gather x7, blocking collectives, cores_gather(): return lax.all_gather(value, 'c', axis=0, tiled=True)  25.8 us
    ppermute x1, starting transfers between devices, swap_cores(): return lax.ppermute(value, 'c', [(0, 1), (1, 0)])  17.4 us
    dot_general x14, matrix products, dot_split(): lax.dot_general(wide, matrix, (((1,), (1,)), ((), ())), preferred_element...  9.65 us
  transfers between devices with their start and end apart: 40, of which 12 were waited for; matrix products, arithmetic and copies ran while one was open for 3% of the time, Pallas kernels for 0%

profile of v5, /device:TPU:1, one launch (start us, length us, event | category | flops | bytes accessed | tf_op | source)
XLA Modules:
  0.0 232.3 jit_solution(8408491713845491637)
XLA Ops:
  0.9 18.9 %collective-permute-start = (f32[64,512]{1,0:T(8,128)S(1)}, f32[64,512]{1,0:T(8,128)S(1)}, u32[]{:S(2)}, u32[]{:S(2)}) collective-permute-start(f32[64,512]{1,0:T(8,128)S(1)} %slice.104), channel_id=1, source_target_pairs={{22,6},{23,7},{24,8},{25,9},{26,10},{27,11},{28,12},{29,13},{38,22... | collective-permute-start | bytes 393224 | tf_op jit(solution)/shard_map/ppermute | solution.py:23
  19.8 17.4 %collective-permute-start.11 = (f32[5,256,512]{2,1,0:T(8,128)}, f32[5,256,512]{2,1,0:T(8,128)}, u32[]{:S(2)}, u32[]{:S(2)}) collective-permute-start(f32[5,256,512]{2,1,0:T(8,128)} %param.4), channel_id=1, source_target_pairs={{0,1},{1,0},{2,3},{3,2},{4,5},{5,4},{6,7},{7,6},{8,9},{9,8},{10,11... | collective-permute-start | bytes 7864328 | tf_op jit(solution)/shard_map/ppermute | solution.py:27
  37.2 1.0 copy.5
  38.2 1.0 slice_select_fusion
  40.6 5.8 %all_gather.21 = f32[512,128]{0,1:T(8,128)S(1)} all-gather(f32[256,128]{0,1:T(8,128)S(1)} %copy.5), channel_id=1, replica_groups=mesh['dom'=32,'y'=8,'c'=2] {'c'}, dimensions={0}, use_global_device_ids=true | all-gather | bytes 393216 | tf_op jit(solution)/shard_map/all_gather | solution.py:31
  49.2 2.2 all_gather.22
  52.7 2.2 all_gather.24
  55.0 2.2 all_gather.25
  57.4 2.2 all_gather.23
  59.8 1.2 fusion.109
  61.0 1.3 collective-permute-start.10
  63.4 1.3 fusion.110
  64.6 1.3 collective-permute-start.7
  65.9 18.2 %collective-permute-done.10 = f32[64,512]{1,0:T(8,128)} collective-permute-done((f32[64,512]{1,0:T(8,128)}, f32[64,512]{1,0:T(8,128)}, u32[]{:S(2)}, u32[]{:S(2)}) %collective-permute-start.10) | collective-permute-done | bytes 131104 | tf_op jit(solution)/shard_map/ppermute | solution.py:23
  84.1 5.6 %collective-permute-done.7 = f32[64,512]{1,0:T(8,128)} collective-permute-done((f32[64,512]{1,0:T(8,128)}, f32[64,512]{1,0:T(8,128)}, u32[]{:S(2)}, u32[]{:S(2)}) %collective-permute-start.7) | collective-permute-done | bytes 131104 | tf_op jit(solution)/shard_map/ppermute | solution.py:23
  89.8 1.0 fusion.93
  90.8 2.2 bitcast_select_fusion.1
  95.6 1.3 collective-permute-start.12
  96.9 1.3 collective-permute-start.13
  98.4 5.1 %collective-permute-done.12 = f32[64,512]{1,0:T(8,128)S(1)} collective-permute-done((f32[64,512]{1,0:T(8,128)S(1)}, f32[64,512]{1,0:T(8,128)S(1)}, u32[]{:S(2)}, u32[]{:S(2)}) %collective-permute-start.12) | collective-permute-done | bytes 131104 | tf_op jit(solution)/shard_map/ppermute | solution.py:23
  103.4 3.8 %collective-permute-done.13 = f32[64,512]{1,0:T(8,128)S(1)} collective-permute-done((f32[64,512]{1,0:T(8,128)S(1)}, f32[64,512]{1,0:T(8,128)S(1)}, u32[]{:S(2)}, u32[]{:S(2)}) %collective-permute-start.13) | collective-permute-done | bytes 131104 | tf_op jit(solution)/shard_map/ppermute | solution.py:23
  109.1 1.3 collective-permute-start.16
  110.4 1.3 collective-permute-start.17
  111.9 6.9 %collective-permute-done.16 = f32[64,512]{1,0:T(8,128)S(1)} collective-permute-done((f32[64,512]{1,0:T(8,128)S(1)}, f32[64,512]{1,0:T(8,128)S(1)}, u32[]{:S(2)}, u32[]{:S(2)}) %collective-permute-start.16) | collective-permute-done | bytes 131104 | tf_op jit(solution)/shard_map/ppermute | solution.py:23
  118.7 5.1 %collective-permute-done.17 = f32[64,512]{1,0:T(8,128)S(1)} collective-permute-done((f32[64,512]{1,0:T(8,128)S(1)}, f32[64,512]{1,0:T(8,128)S(1)}, u32[]{:S(2)}, u32[]{:S(2)}) %collective-permute-start.17) | collective-permute-done | bytes 131104 | tf_op jit(solution)/shard_map/ppermute | solution.py:23
  125.7 1.3 collective-permute-start.23
  127.0 1.3 collective-permute-start.24
  128.5 6.3 %collective-permute-done.23 = f32[64,512]{1,0:T(8,128)S(1)} collective-permute-done((f32[64,512]{1,0:T(8,128)S(1)}, f32[64,512]{1,0:T(8,128)S(1)}, u32[]{:S(2)}, u32[]{:S(2)}) %collective-permute-start.23) | collective-permute-done | bytes 131104 | tf_op jit(solution)/shard_map/ppermute | solution.py:23
  138.1 1.9 collective-permute-start.18
  140.0 4.6 %collective-permute-start.25 = (f32[64,512]{1,0:T(8,128)S(1)}, f32[64,512]{1,0:T(8,128)S(1)}, u32[]{:S(2)}, u32[]{:S(2)}) collective-permute-start(f32[64,512]{1,0:T(8,128)S(1)} %get-tuple-element.6), channel_id=1, source_target_pairs={{0,14},{1,15},{14,0},{15,1},{16,30},{17,31},{30,16},{31,17},{32,46... | collective-permute-start | bytes 393224 | tf_op jit(solution)/shard_map/ppermute | solution.py:23
  146.7 1.9 collective-permute-start.14
  148.7 1.3 collective-permute-start.19
  150.0 1.3 collective-permute-start.26
  152.7 2.9 %collective-permute-done.14 = f32[128,512]{1,0:T(8,128)S(1)} collective-permute-done((f32[128,512]{1,0:T(8,128)S(1)}, f32[128,512]{1,0:T(8,128)S(1)}, u32[]{:S(2)}, u32[]{:S(2)}) %collective-permute-start.14) | collective-permute-done | bytes 262176 | tf_op jit(solution)/shard_map/ppermute | solution.py:23
  155.7 1.9 collective-permute-start.15
  157.6 3.4 %collective-permute-start.20 = (f32[64,512]{1,0:T(8,128)S(1)}, f32[64,512]{1,0:T(8,128)S(1)}, u32[]{:S(2)}, u32[]{:S(2)}) collective-permute-start(f32[64,512]{1,0:T(8,128)S(1)} %add.85), channel_id=1, source_target_pairs={{0,16},{1,17},{14,30},{15,31},{16,0},{17,1},{30,14},{31,15},{32,48... | collective-permute-start | bytes 393224 | tf_op jit(solution)/shard_map/ppermute | solution.py:23
  161.0 1.3 collective-permute-start.27
  162.4 1.3 collective-permute-start.37
  164.4 2.9 %collective-permute-done.27 = f32[64,512]{1,0:T(8,128)S(1)} collective-permute-done((f32[64,512]{1,0:T(8,128)S(1)}, f32[64,512]{1,0:T(8,128)S(1)}, u32[]{:S(2)}, u32[]{:S(2)}) %collective-permute-start.27) | collective-permute-done | bytes 131104 | tf_op jit(solution)/shard_map/ppermute | solution.py:23
  167.3 1.9 collective-permute-start.28
  169.4 3.7 %collective-permute-done.28 = f32[64,512]{1,0:T(8,128)S(1)} collective-permute-done((f32[64,512]{1,0:T(8,128)S(1)}, f32[64,512]{1,0:T(8,128)S(1)}, u32[]{:S(2)}, u32[]{:S(2)}) %collective-permute-start.28) | collective-permute-done | bytes 131104 | tf_op jit(solution)/shard_map/ppermute | solution.py:23
  173.2 1.3 collective-permute-start.38
  174.5 1.3 collective-permute-start.21
  175.8 1.9 collective-permute-done.38
  177.8 23.9 %collective-permute-start.39 = (f32[128,512]{1,0:T(8,128)S(1)}, f32[128,512]{1,0:T(8,128)S(1)}, u32[]{:S(2)}, u32[]{:S(2)}) collective-permute-start(f32[128,512]{1,0:T(8,128)S(1)} %fusion.130), channel_id=1, source_target_pairs={{0,2},{1,3},{4,6},{5,7},{14,12},{15,13},{10,8},{11,9},{16,18},{17,... | collective-permute-start | bytes 786440 | tf_op jit(solution)/shard_map/ppermute | solution.py:23
  201.8 16.1 %collective-permute-start.22 = (f32[192,512]{1,0:T(8,128)S(1)}, f32[192,512]{1,0:T(8,128)S(1)}, u32[]{:S(2)}, u32[]{:S(2)}) collective-permute-start(f32[192,512]{1,0:T(8,128)S(1)} %fusion.132), channel_id=1, source_target_pairs={{0,2},{1,3},{4,6},{5,7},{14,12},{15,13},{10,8},{11,9},{16,18},{17,... | collective-permute-start | bytes 1179656 | tf_op jit(solution)/shard_map/ppermute | solution.py:23
  217.9 6.0 %all_gather.27 = f32[256,512]{1,0:T(8,128)S(1)} all-gather(f32[128,512]{1,0:T(8,128)S(1)} %add.103), channel_id=1, replica_groups=mesh['dom'=32,'y'=8,'c'=2] {'c'}, dimensions={0}, use_global_device_ids=true | all-gather | bytes 786432 | tf_op jit(solution)/shard_map/all_gather | solution.py:31
  224.0 5.3 %all_gather.26 = f32[384,512]{1,0:T(8,128)S(1)} all-gather(f32[192,512]{1,0:T(8,128)S(1)} %add.88), channel_id=1, replica_groups=mesh['dom'=32,'y'=8,'c'=2] {'c'}, dimensions={0}, use_global_device_ids=true | all-gather | bytes 1179648 | tf_op jit(solution)/shard_map/all_gather | solution.py:31
  (133 shorter events, 25.2 us)
Async XLA Ops:
  0.9 37.3 %collective-permute-start = (f32[64,512]{1,0:T(8,128)S(1)}, f32[64,512]{1,0:T(8,128)S(1)}, u32[]{:S(2)}, u32[]{:S(2)}) collective-permute-start(f32[64,512]{1,0:T(8,128)S(1)} %slice.104), channel_id=1, source_target_pairs={{22,6},{23,7},{24,8},{25,9},{26,10},{27,11},{28,12},{29,13},{38,22... | collective-permute-start | bytes 393224 | tf_op jit(solution)/shard_map/ppermute | solution.py:23
  19.8 70.9 %collective-permute-start.11 = (f32[5,256,512]{2,1,0:T(8,128)}, f32[5,256,512]{2,1,0:T(8,128)}, u32[]{:S(2)}, u32[]{:S(2)}) collective-permute-start(f32[5,256,512]{2,1,0:T(8,128)} %param.4), channel_id=1, source_target_pairs={{0,1},{1,0},{2,3},{3,2},{4,5},{5,4},{6,7},{7,6},{8,9},{9,8},{10,11... | collective-permute-start | bytes 7864328 | tf_op jit(solution)/shard_map/ppermute | solution.py:27
  39.2 8.5 %collective-permute-start.2 = (f32[64,512]{1,0:T(8,128)S(1)}, f32[64,512]{1,0:T(8,128)S(1)}, u32[]{:S(2)}, u32[]{:S(2)}) collective-permute-start(f32[64,512]{1,0:T(8,128)S(1)} %get-tuple-element.50), channel_id=1, source_target_pairs={{18,16},{19,17},{10,14},{11,15},{34,32},{35,33},{26,30},{27,31},{5... | collective-permute-start | bytes 393224 | tf_op jit(solution)/shard_map/ppermute | solution.py:23
  39.9 8.5 %collective-permute-start.1 = (f32[64,512]{1,0:T(8,128)S(1)}, f32[64,512]{1,0:T(8,128)S(1)}, u32[]{:S(2)}, u32[]{:S(2)}) collective-permute-start(f32[64,512]{1,0:T(8,128)S(1)} %get-tuple-element.50), channel_id=1, source_target_pairs={{16,16},{17,17},{8,14},{9,15},{32,32},{33,33},{24,30},{25,31},{48,... | collective-permute-start | bytes 393224 | tf_op jit(solution)/shard_map/ppermute | solution.py:23
  46.4 8.5 %collective-permute-start.9 = (f32[64,512]{1,0:T(8,128)S(1)}, f32[64,512]{1,0:T(8,128)S(1)}, u32[]{:S(2)}, u32[]{:S(2)}) collective-permute-start(f32[64,512]{1,0:T(8,128)S(1)} %get-tuple-element.49), channel_id=1, source_target_pairs={{28,16},{29,17},{20,14},{21,15},{44,32},{45,33},{36,30},{37,31},{6... | collective-permute-start | bytes 393224 | tf_op jit(solution)/shard_map/ppermute | solution.py:23
  47.1 7.8 %collective-permute-start.8 = (f32[64,512]{1,0:T(8,128)S(1)}, f32[64,512]{1,0:T(8,128)S(1)}, u32[]{:S(2)}, u32[]{:S(2)}) collective-permute-start(f32[64,512]{1,0:T(8,128)S(1)} %get-tuple-element.49), channel_id=1, source_target_pairs={{26,16},{27,17},{18,14},{19,15},{42,32},{43,33},{34,30},{35,31},{5... | collective-permute-start | bytes 393224 | tf_op jit(solution)/shard_map/ppermute | solution.py:23
  47.8 3.6 %collective-permute-start.6 = (f32[64,512]{1,0:T(8,128)S(1)}, f32[64,512]{1,0:T(8,128)S(1)}, u32[]{:S(2)}, u32[]{:S(2)}) collective-permute-start(f32[64,512]{1,0:T(8,128)S(1)} %get-tuple-element.49), channel_id=1, source_target_pairs={{24,16},{25,17},{16,14},{17,15},{40,32},{41,33},{32,30},{33,31},{5... | collective-permute-start | bytes 393224 | tf_op jit(solution)/shard_map/ppermute | solution.py:23
  48.5 3.6 %collective-permute-start.5 = (f32[64,512]{1,0:T(8,128)S(1)}, f32[64,512]{1,0:T(8,128)S(1)}, u32[]{:S(2)}, u32[]{:S(2)}) collective-permute-start(f32[64,512]{1,0:T(8,128)S(1)} %get-tuple-element.49), channel_id=1, source_target_pairs={{22,16},{23,17},{30,14},{31,15},{38,32},{39,33},{46,30},{47,31},{5... | collective-permute-start | bytes 393224 | tf_op jit(solution)/shard_map/ppermute | solution.py:23
  51.4 5.9 %collective-permute-start.4 = (f32[64,512]{1,0:T(8,128)S(1)}, f32[64,512]{1,0:T(8,128)S(1)}, u32[]{:S(2)}, u32[]{:S(2)}) collective-permute-start(f32[64,512]{1,0:T(8,128)S(1)} %get-tuple-element.50), channel_id=1, source_target_pairs={{30,16},{31,17},{6,14},{7,15},{46,32},{47,33},{22,30},{23,31},{62,... | collective-permute-start | bytes 393224 | tf_op jit(solution)/shard_map/ppermute | solution.py:23
  52.0 5.3 %collective-permute-start.3 = (f32[64,512]{1,0:T(8,128)S(1)}, f32[64,512]{1,0:T(8,128)S(1)}, u32[]{:S(2)}, u32[]{:S(2)}) collective-permute-start(f32[64,512]{1,0:T(8,128)S(1)} %get-tuple-element.50), channel_id=1, source_target_pairs={{20,16},{21,17},{12,14},{13,15},{36,32},{37,33},{28,30},{29,31},{5... | collective-permute-start | bytes 393224 | tf_op jit(solution)/shard_map/ppermute | solution.py:23
  59.8 2.8 %copy-start.1 = (bf16[512,512]{1,0:T(8,128)(2,1)}, bf16[512,512]{1,0:T(8,128)(2,1)S(1)}, u32[]{:S(2)}) copy-start(bf16[512,512]{1,0:T(8,128)(2,1)S(1)} %get-tuple-element.28) | copy-start | bytes 1572868
  61.0 23.1 %collective-permute-start.10 = (f32[64,512]{1,0:T(8,128)}, f32[64,512]{1,0:T(8,128)}, u32[]{:S(2)}, u32[]{:S(2)}) collective-permute-start(f32[64,512]{1,0:T(8,128)} %fusion.109), channel_id=1, source_target_pairs={{16,0},{17,1},{14,30},{15,31},{48,32},{49,33},{46,62},{47,63},{80,... | collective-permute-start | bytes 393224 | tf_op jit(solution)/shard_map/ppermute | solution.py:23
  62.5 0.8 copy-start.3
  62.5 2.1 copy-start.5
  62.6 28.2 %copy-start = (f32[5,256,512]{2,1,0:T(8,128)S(1)}, f32[5,256,512]{2,1,0:T(8,128)}, u32[]{:S(2)}) copy-start(f32[5,256,512]{2,1,0:T(8,128)} %param.4) | copy-start | bytes 7864324
  64.6 25.1 %collective-permute-start.7 = (f32[64,512]{1,0:T(8,128)}, f32[64,512]{1,0:T(8,128)}, u32[]{:S(2)}, u32[]{:S(2)}) collective-permute-start(f32[64,512]{1,0:T(8,128)} %fusion.110), channel_id=1, source_target_pairs={{16,30},{17,31},{14,0},{15,1},{48,62},{49,63},{46,32},{47,33},{80,... | collective-permute-start | bytes 393224 | tf_op jit(solution)/shard_map/ppermute | solution.py:23
  93.2 1.0 copy-start.2
  93.8 1.1 copy-start.4
  93.8 1.2 copy-start.6
  95.6 7.8 %collective-permute-start.12 = (f32[64,512]{1,0:T(8,128)S(1)}, f32[64,512]{1,0:T(8,128)S(1)}, u32[]{:S(2)}, u32[]{:S(2)}) collective-permute-start(f32[64,512]{1,0:T(8,128)S(1)} %fusion.108), channel_id=1, source_target_pairs={{32,62},{33,63},{30,0},{31,1},{96,126},{97,127},{94,64},{95,65},{1... | collective-permute-start | bytes 393224 | tf_op jit(solution)/shard_map/ppermute | solution.py:23
  96.9 10.4 %collective-permute-start.13 = (f32[64,512]{1,0:T(8,128)S(1)}, f32[64,512]{1,0:T(8,128)S(1)}, u32[]{:S(2)}, u32[]{:S(2)}) collective-permute-start(f32[64,512]{1,0:T(8,128)S(1)} %fusion.107), channel_id=1, source_target_pairs={{32,0},{33,1},{30,62},{31,63},{96,64},{97,65},{94,126},{95,127},{1... | collective-permute-start | bytes 393224 | tf_op jit(solution)/shard_map/ppermute | solution.py:23
  109.1 9.6 %collective-permute-start.16 = (f32[64,512]{1,0:T(8,128)S(1)}, f32[64,512]{1,0:T(8,128)S(1)}, u32[]{:S(2)}, u32[]{:S(2)}) collective-permute-start(f32[64,512]{1,0:T(8,128)S(1)} %fusion.106), channel_id=1, source_target_pairs={{64,126},{65,127},{62,0},{63,1},{192,254},{193,255},{190,128},{191... | collective-permute-start | bytes 393224 | tf_op jit(solution)/shard_map/ppermute | solution.py:23
  110.4 13.4 %collective-permute-start.17 = (f32[64,512]{1,0:T(8,128)S(1)}, f32[64,512]{1,0:T(8,128)S(1)}, u32[]{:S(2)}, u32[]{:S(2)}) collective-permute-start(f32[64,512]{1,0:T(8,128)S(1)} %fusion.105), channel_id=1, source_target_pairs={{64,0},{65,1},{62,126},{63,127},{192,128},{193,129},{190,254},{191... | collective-permute-start | bytes 393224 | tf_op jit(solution)/shard_map/ppermute | solution.py:23
  125.7 9.0 %collective-permute-start.23 = (f32[64,512]{1,0:T(8,128)S(1)}, f32[64,512]{1,0:T(8,128)S(1)}, u32[]{:S(2)}, u32[]{:S(2)}) collective-permute-start(f32[64,512]{1,0:T(8,128)S(1)} %fusion.104), channel_id=1, source_target_pairs={{128,254},{129,255},{126,0},{127,1},{384,510},{385,511},{382,256},... | collective-permute-start | bytes 393224 | tf_op jit(solution)/shard_map/ppermute | solution.py:23
  127.0 7.9 %collective-permute-start.24 = (f32[64,512]{1,0:T(8,128)S(1)}, f32[64,512]{1,0:T(8,128)S(1)}, u32[]{:S(2)}, u32[]{:S(2)}) collective-permute-start(f32[64,512]{1,0:T(8,128)S(1)} %fusion.103), channel_id=1, source_target_pairs={{128,0},{129,1},{126,254},{127,255},{384,256},{385,257},{382,510},... | collective-permute-start | bytes 393224 | tf_op jit(solution)/shard_map/ppermute | solution.py:23
  136.7 7.9 %collective-permute-start.29 = (f32[64,512]{1,0:T(8,128)S(1)}, f32[64,512]{1,0:T(8,128)S(1)}, u32[]{:S(2)}, u32[]{:S(2)}) collective-permute-start(f32[64,512]{1,0:T(8,128)S(1)} %fusion.102), channel_id=1, source_target_pairs={{256,270},{257,271},{254,240},{255,241}} | collective-permute-start | bytes 393224 | tf_op jit(solution)/shard_map/ppermute | solution.py:23
  137.4 7.2 %collective-permute-start.30 = (f32[64,512]{1,0:T(8,128)S(1)}, f32[64,512]{1,0:T(8,128)S(1)}, u32[]{:S(2)}, u32[]{:S(2)}) collective-permute-start(f32[64,512]{1,0:T(8,128)S(1)} %fusion.101), channel_id=1, source_target_pairs={{256,240},{257,241},{254,270},{255,271}} | collective-permute-start | bytes 393224 | tf_op jit(solution)/shard_map/ppermute | solution.py:23
  138.1 8.6 %collective-permute-start.18 = (f32[64,512]{1,0:T(8,128)S(1)}, f32[64,512]{1,0:T(8,128)S(1)}, u32[]{:S(2)}, u32[]{:S(2)}) collective-permute-start(f32[64,512]{1,0:T(8,128)S(1)} %get-tuple-element.8), channel_id=1, source_target_pairs={{0,14},{1,15},{14,0},{15,1},{16,30},{17,31},{30,16},{31,17},{32,46... | collective-permute-start | bytes 393224 | tf_op jit(solution)/shard_map/ppermute | solution.py:23
  140.0 8.7 %collective-permute-start.25 = (f32[64,512]{1,0:T(8,128)S(1)}, f32[64,512]{1,0:T(8,128)S(1)}, u32[]{:S(2)}, u32[]{:S(2)}) collective-permute-start(f32[64,512]{1,0:T(8,128)S(1)} %get-tuple-element.6), channel_id=1, source_target_pairs={{0,14},{1,15},{14,0},{15,1},{16,30},{17,31},{30,16},{31,17},{32,46... | collective-permute-start | bytes 393224 | tf_op jit(solution)/shard_map/ppermute | solution.py:23
  144.6 5.4 %collective-permute-start.33 = (f32[64,512]{1,0:T(8,128)S(1)}, f32[64,512]{1,0:T(8,128)S(1)}, u32[]{:S(2)}, u32[]{:S(2)}) collective-permute-start(f32[64,512]{1,0:T(8,128)S(1)} %add.94), channel_id=1, source_target_pairs={{270,256},{271,257},{240,254},{241,255}} | collective-permute-start | bytes 393224 | tf_op jit(solution)/shard_map/ppermute | solution.py:23
  145.3 6.0 %collective-permute-start.32 = (f32[64,512]{1,0:T(8,128)S(1)}, f32[64,512]{1,0:T(8,128)S(1)}, u32[]{:S(2)}, u32[]{:S(2)}) collective-permute-start(f32[64,512]{1,0:T(8,128)S(1)} %add.94), channel_id=1, source_target_pairs={{270,398},{271,399},{240,112},{241,113}} | collective-permute-start | bytes 393224 | tf_op jit(solution)/shard_map/ppermute | solution.py:23
  146.0 5.3 %collective-permute-start.31 = (f32[64,512]{1,0:T(8,128)S(1)}, f32[64,512]{1,0:T(8,128)S(1)}, u32[]{:S(2)}, u32[]{:S(2)}) collective-permute-start(f32[64,512]{1,0:T(8,128)S(1)} %add.94), channel_id=1, source_target_pairs={{270,384},{271,385},{240,126},{241,127}} | collective-permute-start | bytes 393224 | tf_op jit(solution)/shard_map/ppermute | solution.py:23
  146.7 8.9 %collective-permute-start.14 = (f32[128,512]{1,0:T(8,128)S(1)}, f32[128,512]{1,0:T(8,128)S(1)}, u32[]{:S(2)}, u32[]{:S(2)}) collective-permute-start(f32[128,512]{1,0:T(8,128)S(1)} %pad_maximum_fusion.11), channel_id=1, source_target_pairs={{0,14},{1,15},{14,0},{15,1},{16,30},{17,31},{30,16},{31,17},{32,46... | collective-permute-start | bytes 786440 | tf_op jit(solution)/shard_map/ppermute | solution.py:23
  148.7 8.9 %collective-permute-start.19 = (f32[64,512]{1,0:T(8,128)S(1)}, f32[64,512]{1,0:T(8,128)S(1)}, u32[]{:S(2)}, u32[]{:S(2)}) collective-permute-start(f32[64,512]{1,0:T(8,128)S(1)} %add.84), channel_id=1, source_target_pairs={{0,32},{1,33},{14,46},{15,47},{112,80},{113,81},{126,94},{127,95},... | collective-permute-start | bytes 393224 | tf_op jit(solution)/shard_map/ppermute | solution.py:23
  150.0 11.0 %collective-permute-start.26 = (f32[64,512]{1,0:T(8,128)S(1)}, f32[64,512]{1,0:T(8,128)S(1)}, u32[]{:S(2)}, u32[]{:S(2)}) collective-permute-start(f32[64,512]{1,0:T(8,128)S(1)} %add.90), channel_id=1, source_target_pairs={{0,64},{1,65},{14,78},{15,79},{240,176},{241,177},{254,190},{255,1... | collective-permute-start | bytes 393224 | tf_op jit(solution)/shard_map/ppermute | solution.py:23
  151.4 11.0 %collective-permute-start.35 = (f32[64,512]{1,0:T(8,128)S(1)}, f32[64,512]{1,0:T(8,128)S(1)}, u32[]{:S(2)}, u32[]{:S(2)}) collective-permute-start(f32[64,512]{1,0:T(8,128)S(1)} %add_add_fusion.2), channel_id=1, source_target_pairs={{112,32},{113,33},{126,46},{127,47},{240,160},{241,161},{254,174},... | collective-permute-start | bytes 393224 | tf_op jit(solution)/shard_map/ppermute | solution.py:23
  152.0 10.3 %collective-permute-start.34 = (f32[64,512]{1,0:T(8,128)S(1)}, f32[64,512]{1,0:T(8,128)S(1)}, u32[]{:S(2)}, u32[]{:S(2)}) collective-permute-start(f32[64,512]{1,0:T(8,128)S(1)} %add_add_fusion.2), channel_id=1, source_target_pairs={{112,64},{113,65},{126,78},{127,79},{240,192},{241,193},{254,206},... | collective-permute-start | bytes 393224 | tf_op jit(solution)/shard_map/ppermute | solution.py:23
  155.7 13.6 %collective-permute-start.15 = (f32[64,512]{1,0:T(8,128)S(1)}, f32[64,512]{1,0:T(8,128)S(1)}, u32[]{:S(2)}, u32[]{:S(2)}) collective-permute-start(f32[64,512]{1,0:T(8,128)S(1)} %slice.108), channel_id=1, source_target_pairs={{0,16},{1,17},{14,30},{15,31},{16,0},{17,1},{30,14},{31,15},{32,48... | collective-permute-start | bytes 393224 | tf_op jit(solution)/shard_map/ppermute | solution.py:23
  157.6 11.7 %collective-permute-start.20 = (f32[64,512]{1,0:T(8,128)S(1)}, f32[64,512]{1,0:T(8,128)S(1)}, u32[]{:S(2)}, u32[]{:S(2)}) collective-permute-start(f32[64,512]{1,0:T(8,128)S(1)} %add.85), channel_id=1, source_target_pairs={{0,16},{1,17},{14,30},{15,31},{16,0},{17,1},{30,14},{31,15},{32,48... | collective-permute-start | bytes 393224 | tf_op jit(solution)/shard_map/ppermute | solution.py:23
  161.0 6.3 %collective-permute-start.27 = (f32[64,512]{1,0:T(8,128)S(1)}, f32[64,512]{1,0:T(8,128)S(1)}, u32[]{:S(2)}, u32[]{:S(2)}) collective-permute-start(f32[64,512]{1,0:T(8,128)S(1)} %add.91), channel_id=1, source_target_pairs={{0,32},{1,33},{14,46},{15,47},{64,96},{65,97},{78,110},{79,111},{1... | collective-permute-start | bytes 393224 | tf_op jit(solution)/shard_map/ppermute | solution.py:23
  162.4 10.7 %collective-permute-start.37 = (f32[64,512]{1,0:T(8,128)S(1)}, f32[64,512]{1,0:T(8,128)S(1)}, u32[]{:S(2)}, u32[]{:S(2)}) collective-permute-start(f32[64,512]{1,0:T(8,128)S(1)} %add_add_fusion.1), channel_id=1, source_target_pairs={{112,0},{113,1},{126,14},{127,15},{64,80},{65,81},{78,94},{79,95},... | collective-permute-start | bytes 393224 | tf_op jit(solution)/shard_map/ppermute | solution.py:23
  163.7 9.4 %collective-permute-start.36 = (f32[64,512]{1,0:T(8,128)S(1)}, f32[64,512]{1,0:T(8,128)S(1)}, u32[]{:S(2)}, u32[]{:S(2)}) collective-permute-start(f32[64,512]{1,0:T(8,128)S(1)} %add_add_fusion.1), channel_id=1, source_target_pairs={{112,96},{113,97},{126,110},{127,111},{64,48},{65,49},{78,62},{79,... | collective-permute-start | bytes 393224 | tf_op jit(solution)/shard_map/ppermute | solution.py:23
  167.3 5.7 %collective-permute-start.28 = (f32[64,512]{1,0:T(8,128)S(1)}, f32[64,512]{1,0:T(8,128)S(1)}, u32[]{:S(2)}, u32[]{:S(2)}) collective-permute-start(f32[64,512]{1,0:T(8,128)S(1)} %add.92), channel_id=1, source_target_pairs={{0,16},{1,17},{14,30},{15,31},{16,0},{17,1},{30,14},{31,15},{32,48... | collective-permute-start | bytes 393224 | tf_op jit(solution)/shard_map/ppermute | solution.py:23
  173.2 4.6 %collective-permute-start.38 = (f32[128,512]{1,0:T(8,128)S(1)}, f32[128,512]{1,0:T(8,128)S(1)}, u32[]{:S(2)}, u32[]{:S(2)}) collective-permute-start(f32[128,512]{1,0:T(8,128)S(1)} %pad_maximum_fusion.12), channel_id=1, source_target_pairs={{0,4},{1,5},{14,10},{15,11},{16,20},{17,21},{30,26},{31,27},{32,36... | collective-permute-start | bytes 786440 | tf_op jit(solution)/shard_map/ppermute | solution.py:23
  174.5 27.2 %collective-permute-start.21 = (f32[192,512]{1,0:T(8,128)S(1)}, f32[192,512]{1,0:T(8,128)S(1)}, u32[]{:S(2)}, u32[]{:S(2)}) collective-permute-start(f32[192,512]{1,0:T(8,128)S(1)} %pad_maximum_fusion.6), channel_id=1, source_target_pairs={{0,4},{1,5},{14,10},{15,11},{16,20},{17,21},{30,26},{31,27},{32,36... | collective-permute-start | bytes 1179656 | tf_op jit(solution)/shard_map/ppermute | solution.py:23
  177.8 40.1 %collective-permute-start.39 = (f32[128,512]{1,0:T(8,128)S(1)}, f32[128,512]{1,0:T(8,128)S(1)}, u32[]{:S(2)}, u32[]{:S(2)}) collective-permute-start(f32[128,512]{1,0:T(8,128)S(1)} %fusion.130), channel_id=1, source_target_pairs={{0,2},{1,3},{4,6},{5,7},{14,12},{15,13},{10,8},{11,9},{16,18},{17,... | collective-permute-start | bytes 786440 | tf_op jit(solution)/shard_map/ppermute | solution.py:23
  201.8 22.2 %collective-permute-start.22 = (f32[192,512]{1,0:T(8,128)S(1)}, f32[192,512]{1,0:T(8,128)S(1)}, u32[]{:S(2)}, u32[]{:S(2)}) collective-permute-start(f32[192,512]{1,0:T(8,128)S(1)} %fusion.132), channel_id=1, source_target_pairs={{0,2},{1,3},{4,6},{5,7},{14,12},{15,13},{10,8},{11,9},{16,18},{17,... | collective-permute-start | bytes 1179656 | tf_op jit(solution)/shard_map/ppermute | solution.py:23
